TPU v7x, 32 devices: a whole 2x2x4 slice. The times are simulated.
32 devices in a mesh: dp: 16 (over z, x, core), tensor: 2 (over y).
Axes of the slice: x: 2, y: 2, z: 4, core: 2. Of those that a mesh axis runs over, the one named last changes fastest.
Arguments:
- inputs: bfloat16 [12288, 768], P('dp'), may hold values from -6 to 6
- clip_ids: int32 [12288], replicated, may hold values from 0 to 11, never falling along the last dimension, each value on 1 to 1500 neighbouring positions
- attn_gain: bfloat16 [768], replicated, may hold values from 0.5 to 1.5
- attn_shift: bfloat16 [768], replicated, may hold values from -1.75 to 1.75
- w_query: bfloat16 [768, 768], P(None, 'tensor'), may hold values from -0.21875 to 0.21875
- query_bias: bfloat16 [768], P('tensor'), may hold values from -1.75 to 1.75
- w_key: bfloat16 [768, 768], P(None, 'tensor'), may hold values from -0.21875 to 0.21875
- w_value: bfloat16 [768, 768], P(None, 'tensor'), may hold values from -0.21875 to 0.21875
- value_bias: bfloat16 [768], P('tensor'), may hold values from -3 to 3
- w_out: bfloat16 [768, 768], P('tensor'), may hold values from -4 to 4
- out_bias: bfloat16 [768], replicated, may hold values from -1.75 to 1.75
- mlp_gain: bfloat16 [768], replicated, may hold values from 0.5 to 1.5
- mlp_shift: bfloat16 [768], replicated, may hold values from -1.75 to 1.75
- w_fc1: bfloat16 [768, 3072], P(None, 'tensor'), may hold values from -0.21875 to 0.21875
- fc1_bias: bfloat16 [3072], P('tensor'), may hold values from -3 to 3
- w_fc2: bfloat16 [3072, 768], P('tensor'), may hold values from -0.109375 to 0.109375
- fc2_bias: bfloat16 [768], replicated, may hold values from -1.75 to 1.75
- cotangent: bfloat16 [12288, 768], P('dp'), may hold values from -6 to 6
Outputs:
- layer_out: bfloat16 [12288, 768], P('dp')
- inputs_grad: float32 [12288, 768], P('dp')
- attn_gain_grad: float32 [768], replicated
- attn_shift_grad: float32 [768], replicated
- w_query_grad: float32 [768, 768], P(None, 'tensor')
- query_bias_grad: float32 [768], P('tensor')
- w_key_grad: float32 [768, 768], P(None, 'tensor')
- w_value_grad: float32 [768, 768], P(None, 'tensor')
- value_bias_grad: float32 [768], P('tensor')
- w_out_grad: float32 [768, 768], P('tensor')
- out_bias_grad: float32 [768], replicated
- mlp_gain_grad: float32 [768], replicated
- mlp_shift_grad: float32 [768], replicated
- w_fc1_grad: float32 [768, 3072], P(None, 'tensor')
- fc1_bias_grad: float32 [3072], P('tensor')
- w_fc2_grad: float32 [3072, 768], P('tensor')
- fc2_bias_grad: float32 [768], replicated
Inputs may be any that keep to these rules, and one draw needn't show every extreme that they name: `clip_ids`: clip numbers never fall along the tokens; each of the 12 clips holds 1 to 1500 consecutive tokens, and one holds exactly 1500.
All inputs are finite; a program needn't handle non-finite values.
Results may differ from a plain program's by a relative error of at most 0.012.
Values may be sent and summed in bfloat16 or wider, within the bound.
A program may use at most 128 MiB of HBM per device.

v0:
```python
import jax
import jax.numpy as jnp
from jax import lax
from jax.sharding import PartitionSpec as P

HEAD_DIM = 64
REACH = 2


def from_behind(block, axis, distance):
    devices = range(lax.axis_size(axis))
    route = [(i - distance, i) for i in devices if i - distance in devices]
    return lax.ppermute(block, axis, route)


def layer_norm(values, gain_row, bias_row):
    middle = jnp.mean(values, axis=-1, keepdims=True)
    centred = values - middle
    spread = jnp.mean(centred * centred, axis=-1, keepdims=True)
    return centred * lax.rsqrt(spread + 1e-05) * gain_row + bias_row


def exact_gelu(values):
    return jax.nn.gelu(values, approximate=False)


def matmul(left, right):
    return jnp.dot(left, right, preferred_element_type=jnp.float32)


def contract_rows(left, right):
    return lax.dot_general(
        left, right, (((0,), (0,)), ((), ())), preferred_element_type=jnp.float32
    )


def contract_cols(left, right):
    return lax.dot_general(
        left, right, (((1,), (1,)), ((), ())), preferred_element_type=jnp.float32
    )


def split_heads(values):
    return values.reshape(values.shape[0], values.shape[1] // HEAD_DIM, HEAD_DIM).transpose(1, 0, 2)


def join_heads(stacked):
    return stacked.transpose(1, 0, 2).reshape(stacked.shape[1], stacked.shape[0] * stacked.shape[2])


def on_device(
    inputs,
    clip_ids,
    attn_gain,
    attn_shift,
    w_query,
    query_bias,
    w_key,
    w_value,
    value_bias,
    w_out,
    out_bias,
    mlp_gain,
    mlp_shift,
    w_fc1,
    fc1_bias,
    w_fc2,
    fc2_bias,
    cotangent,
):
    height = inputs.shape[0]
    devices = lax.axis_size("dp")
    myself = lax.axis_index("dp")
    factor = HEAD_DIM ** (-0.5)
    offsets = list(range(-REACH, REACH + 1))

    def clip_block(offset):
        holder = myself + offset
        begin_at = jnp.clip(holder, 0, devices - 1) * height
        labels = lax.dynamic_slice_in_dim(clip_ids, begin_at, height)
        inside = jnp.logical_and(holder >= 0, holder < devices)
        return jnp.where(inside, labels, -1)

    own_labels = clip_block(0)
    key_labels = jnp.concatenate([clip_block(offset) for offset in offsets])
    allowed = own_labels[:, None] == key_labels[None, :]
    source = inputs.astype(jnp.float32)
    normed_one, norm_one_back = jax.vjp(
        layer_norm, source, attn_gain.astype(jnp.float32), attn_shift.astype(jnp.float32)
    )
    attn_input = normed_one.astype(jnp.bfloat16)
    queries = (matmul(attn_input, w_query) + query_bias.astype(jnp.float32)).astype(jnp.bfloat16)
    keys_own = matmul(attn_input, w_key).astype(jnp.bfloat16)
    values_own = (matmul(attn_input, w_value) + value_bias.astype(jnp.float32)).astype(jnp.bfloat16)
    key_parts = []
    value_parts = []
    for offset in offsets:
        if offset == 0:
            key_parts.append(keys_own)
            value_parts.append(values_own)
        else:
            moved_keys, moved_values = from_behind((keys_own, values_own), "dp", -offset)
            key_parts.append(moved_keys)
            value_parts.append(moved_values)
    query_heads = split_heads(queries)
    key_heads = split_heads(jnp.concatenate(key_parts))
    value_heads = split_heads(jnp.concatenate(value_parts))

    def attend(operands):
        query_one, key_one, value_one = operands
        scores = jnp.where(allowed, contract_cols(query_one, key_one) * factor, -1e30)
        largest = jnp.max(scores, axis=1, keepdims=True)
        expset = jnp.exp(scores - largest)
        totals = jnp.sum(expset, axis=1, keepdims=True)
        weights = (expset / totals).astype(jnp.bfloat16)
        mixed_one = matmul(weights, value_one)
        return (mixed_one.astype(jnp.bfloat16), largest[:, 0] + jnp.log(totals[:, 0]))

    head_out, log_totals = lax.map(attend, (query_heads, key_heads, value_heads))
    attn_mixed = join_heads(head_out)
    attn_total = lax.psum(matmul(attn_mixed, w_out), "tensor") + out_bias.astype(jnp.float32)
    residual = source + attn_total
    normed_two, norm_two_back = jax.vjp(
        layer_norm, residual, mlp_gain.astype(jnp.float32), mlp_shift.astype(jnp.float32)
    )
    mlp_input = normed_two.astype(jnp.bfloat16)
    preact = matmul(mlp_input, w_fc1) + fc1_bias.astype(jnp.float32)
    activated_full, gelu_back = jax.vjp(exact_gelu, preact)
    activated = activated_full.astype(jnp.bfloat16)
    mlp_total = lax.psum(matmul(activated, w_fc2).astype(jnp.bfloat16), "tensor").astype(
        jnp.float32
    ) + fc2_bias.astype(jnp.float32)
    layer_out = (residual + mlp_total).astype(jnp.bfloat16)
    out_grad_full = cotangent.astype(jnp.float32)
    fc2_bias_grad = jnp.sum(out_grad_full, axis=0)
    w_fc2_grad = contract_rows(activated, cotangent)
    (pre_full,) = gelu_back(contract_cols(cotangent, w_fc2))
    pre_grad = pre_full.astype(jnp.bfloat16)
    fc1_bias_grad = jnp.sum(pre_grad.astype(jnp.float32), axis=0)
    w_fc1_grad = contract_rows(mlp_input, pre_grad)
    mlp_in_grad = lax.psum(contract_cols(pre_grad, w_fc1), "tensor")
    resid_back, mlp_gain_grad, mlp_shift_grad = norm_two_back(mlp_in_grad)
    residual_grad = out_grad_full + resid_back
    attn_grad_low = residual_grad.astype(jnp.bfloat16)
    out_bias_grad = jnp.sum(attn_grad_low.astype(jnp.float32), axis=0)
    w_out_grad = contract_rows(attn_mixed, attn_grad_low)
    mixed_heads = split_heads(contract_cols(attn_grad_low, w_out).astype(jnp.bfloat16))

    def attend_back(operands):
        query_one, key_one, value_one, log_total, mixed_one = operands
        scores = jnp.where(allowed, contract_cols(query_one, key_one) * factor, -1e30)
        probs = jnp.exp(scores - log_total[:, None])
        probs_low = probs.astype(jnp.bfloat16)
        prob_grad = contract_cols(mixed_one, value_one)
        centre = jnp.sum(probs * prob_grad, axis=1, keepdims=True)
        score_grad = (probs * (prob_grad - centre)).astype(jnp.bfloat16)
        query_part = (matmul(score_grad, key_one) * factor).astype(jnp.bfloat16)
        key_part = contract_rows(score_grad, query_one) * factor
        value_part = contract_rows(probs_low, mixed_one)
        return (query_part, key_part, value_part)

    query_parts, key_grads, value_grads = lax.map(
        attend_back, (query_heads, key_heads, value_heads, log_totals, mixed_heads)
    )
    query_low = join_heads(query_parts)
    key_window_grad = join_heads(key_grads)
    value_window_grad = join_heads(value_grads)
    centre_row = REACH * height
    key_sum = key_window_grad[centre_row : centre_row + height]
    value_sum = value_window_grad[centre_row : centre_row + height]
    for position, offset in enumerate(offsets):
        if offset != 0:
            begin_row = position * height
            back_keys, back_values = (
                from_behind(
                    key_window_grad[begin_row : begin_row + height].astype(jnp.bfloat16),
                    "dp",
                    offset,
                ).astype(jnp.float32),
                from_behind(
                    value_window_grad[begin_row : begin_row + height].astype(jnp.bfloat16),
                    "dp",
                    offset,
                ).astype(jnp.float32),
            )
            key_sum = key_sum + back_keys
            value_sum = value_sum + back_values
    key_low = key_sum.astype(jnp.bfloat16)
    value_low = value_sum.astype(jnp.bfloat16)
    query_bias_grad = jnp.sum(query_low.astype(jnp.float32), axis=0)
    value_bias_grad = jnp.sum(value_low.astype(jnp.float32), axis=0)
    w_query_grad = contract_rows(attn_input, query_low)
    w_key_grad = contract_rows(attn_input, key_low)
    w_value_grad = contract_rows(attn_input, value_low)
    attn_in_part = (
        contract_cols(query_low, w_query)
        + contract_cols(key_low, w_key)
        + contract_cols(value_low, w_value)
    )
    attn_in_grad = lax.psum(attn_in_part.astype(jnp.bfloat16), "tensor").astype(jnp.float32)
    source_back, attn_gain_grad, attn_shift_grad = norm_one_back(attn_in_grad)
    inputs_grad = residual_grad + source_back
    (
        w_query_grad,
        query_bias_grad,
        w_key_grad,
        w_value_grad,
        value_bias_grad,
        w_out_grad,
        out_bias_grad,
        attn_gain_grad,
        attn_shift_grad,
        w_fc1_grad,
        fc1_bias_grad,
        w_fc2_grad,
        fc2_bias_grad,
        mlp_gain_grad,
        mlp_shift_grad,
    ) = lax.psum(
        (
            w_query_grad,
            query_bias_grad,
            w_key_grad,
            w_value_grad,
            value_bias_grad,
            w_out_grad,
            out_bias_grad,
            attn_gain_grad,
            attn_shift_grad,
            w_fc1_grad,
            fc1_bias_grad,
            w_fc2_grad,
            fc2_bias_grad,
            mlp_gain_grad,
            mlp_shift_grad,
        ),
        "dp",
    )
    return (
        layer_out,
        inputs_grad,
        attn_gain_grad,
        attn_shift_grad,
        w_query_grad,
        query_bias_grad,
        w_key_grad,
        w_value_grad,
        value_bias_grad,
        w_out_grad,
        out_bias_grad,
        mlp_gain_grad,
        mlp_shift_grad,
        w_fc1_grad,
        fc1_bias_grad,
        w_fc2_grad,
        fc2_bias_grad,
    )


def solution(mesh):
    in_specs = (
        P("dp", None),
        P(),
        P(),
        P(),
        P(None, "tensor"),
        P("tensor"),
        P(None, "tensor"),
        P(None, "tensor"),
        P("tensor"),
        P("tensor", None),
        P(),
        P(),
        P(),
        P(None, "tensor"),
        P("tensor"),
        P("tensor", None),
        P(),
        P("dp", None),
    )
    out_specs = (
        P("dp", None),
        P("dp", None),
        P(),
        P(),
        P(None, "tensor"),
        P("tensor"),
        P(None, "tensor"),
        P(None, "tensor"),
        P("tensor"),
        P("tensor", None),
        P(),
        P(),
        P(),
        P(None, "tensor"),
        P("tensor"),
        P("tensor", None),
        P(),
    )
    return jax.shard_map(
        on_device, mesh=mesh, in_specs=in_specs, out_specs=out_specs, check_vma=False
    )
```

profile of v0, /device:TPU:0, one launch (start us, length us, event | category | flops | bytes accessed | tf_op | source)
XLA Modules:
  0.0 940.8 jit_solution(11370151416153895606)
XLA Ops:
  15.0 5.8 collective-permute-start
  27.3 6.1 collective-permute-start.4
  44.1 8.9 collective-permute-done
  72.0 6.5 copy.42
  94.9 6.5 copy.43
  102.2 65.1 %while.28 = (s32[]{:T(128)}, bf16[6,768,64]{1,2,0:T(8,128)(2,1)}, f32[6,768]{1,0:T(8,128)}, bf16[6,768,64]{2,1,0:T(8,128)(2,1)}, bf16[6,3840,64]{2,1,0:T(8,128)(...) while((s32[]{:T(128)}, bf16[6,768,64]{1,2,0:T(8,128)(2,1)}, ...), condition=%wide.region_5.6_spmd.clone, body=%wide.region_2.5_spmd.clone.sunk | while | flops 781565184 | bytes 37708912 | solution.py:119
  173.7 80.5 %all-reduce.8.cloned.1.call-done = f32[768,768]{1,0:T(8,128)} async-done(((f32[768,768]{1,0:T(8,128)}), f32[768,768]{1,0:T(8,128)}) %all-reduce.8.cloned.1.call-update) | async-done | bytes 2359312 | tf_op jit(solution)/shard_map/psum | solution.py:121
  261.1 14.3 %convert_reduce_fusion = (f32[1536]{0:T(1024)}, bf16[768,1536]{1,0:T(8,128)(2,1)S(1)}, f32[768,1536]{1,0:T(8,128)}) fusion(f32[768,1536]{1,0:T(8,128)S(1)} %fusion.82, f32[1536]{0:T(1024)S(1)} %copy-done.53, bf16[768,768]{1,0:T(8,128)(2,1)S(1)} %copy-done.18, bf16[1536,768]{1,0:T(8,128)(2,1)S(1)} %copy-done), kind=kOutput, calls=%fused_computation.56 | convolution fusion | flops 1900411392 | bytes 15347712 | tf_op jit(solution)/shard_map/dot_general | solution.py:38
  289.6 59.4 %all-reduce.10.cloned.1.call-done = f32[768,768]{1,0:T(8,128)} async-done(((f32[768,768]{1,0:T(8,128)}), f32[768,768]{1,0:T(8,128)}) %all-reduce.10.cloned.1.call-update) | async-done | bytes 2359312 | tf_op jit(solution)/shard_map/psum | solution.py:141
  357.5 137.6 %while.29 = (s32[]{:T(128)}, bf16[6,768,64]{1,2,0:T(8,128)(2,1)S(1)}, f32[6,3840,64]{1,2,0:T(8,128)}, f32[6,3840,64]{1,2,0:T(8,128)}, bf16[6,768,64]{2,1,0:T(8,1...) while((s32[]{:T(128)}, ...), condition=%wide.region_15.16_spmd.clone, body=%wide.region_13.15_spmd.clone.sunk | while | flops 1917271296 | bytes 117906592 | solution.py:162
  370.2 5.0 fusion.165
  393.1 5.0 fusion.165
  416.1 5.0 fusion.165
  439.0 5.0 fusion.165
  484.8 5.0 fusion.165
  496.7 5.1 bitcast_convert_fusion
  509.9 6.9 collective-permute-start.15
  519.0 19.1 %collective-permute-done.11 = bf16[768,384]{0,1:T(8,128)(2,1)S(1)} collective-permute-done((bf16[768,384]{0,1:T(8,128)(2,1)S(1)}, bf16[768,384]{0,1:T(8,128)(2,1)S(1)}, u32[]{:S(2)}, u32[]{:S(2)}) %collective-permute-start.11) | collective-permute-done | bytes 589856 | tf_op jit(solution)/shard_map/ppermute | solution.py:13
  543.4 13.6 %collective-permute-done.15 = bf16[768,384]{0,1:T(8,128)(2,1)S(1)} collective-permute-done((bf16[768,384]{0,1:T(8,128)(2,1)S(1)}, bf16[768,384]{0,1:T(8,128)(2,1)S(1)}, u32[]{:S(2)}, u32[]{:S(2)}) %collective-permute-start.15) | collective-permute-done | bytes 589856 | tf_op jit(solution)/shard_map/ppermute | solution.py:13
  558.3 21.4 %collective-permute-done.12 = bf16[768,384]{0,1:T(8,128)(2,1)S(1)} collective-permute-done((bf16[768,384]{0,1:T(8,128)(2,1)S(1)}, bf16[768,384]{0,1:T(8,128)(2,1)S(1)}, u32[]{:S(2)}, u32[]{:S(2)}) %collective-permute-start.12) | collective-permute-done | bytes 589856 | tf_op jit(solution)/shard_map/ppermute | solution.py:13
  582.8 6.4 fusion.99
  605.5 48.7 %all-reduce.14.cloned.1.call-done = (bf16[768,768]{1,0:T(8,128)(2,1)}, bf16[768,768]{1,0:T(8,128)(2,1)}) async-done(((bf16[768,768]{1,0:T(8,128)(2,1)}, bf16[768,768]{1,0:T(8,128)(2,1)}), (bf16[768,768]{1,0:T(8,128)(2,1)}, bf16[768,768]{1,0:T(8,128)(2,1)})) %all-reduce.14.cloned.1.call-update) | async-done | bytes 2359312 | tf_op jit(solution)/shard_map/psum | solution.py:130
  662.0 65.9 %all-reduce = (f32[768]{0:T(1024)}, f32[768]{0:T(1024)}, f32[384]{0:T(512)}, f32[384]{0:T(512)}, f32[768]{0:T(1024)}, /*index=5*/f32[768]{0:T(1024)}, f32[768]{0:T(1024)}, f32[1536]{0:T(1024)}, f32[768]{0:T(1024)}) all-reduce(f32[768]{0:T(1024)} %get-tuple-element.181, ...), channel_id=1, replica_groups=mesh['dp'=16,'tensor'=2] {'dp'}, use_global_device_ids=true, to_apply=%region_20.21 | all-reduce | flops 6912 | bytes 55296 | tf_op jit(solution)/shard_map/psum | solution.py:219
  730.5 191.6 %all-reduce.12.cloned.1.call-done = (f32[768,384]{1,0:T(8,128)}, f32[768,384]{1,0:T(8,128)}, f32[768,384]{1,0:T(8,128)}, f32[384,768]{1,0:T(8,128)}, f32[768,1536]{1,0:T(8,128)}, /*index=5*/f32[1536,768]{1,0:T(8,128)}) async-done(((f32[768,384]{1,0:T(8,128)}, f32[768,384]{1,0:T(8,128)}, f32[768,384]{1,0:T(8,128)}, f32[384,768]{1,0:T(8,128)}, f32[768,1536]{1,0:T(8,128)}, /*index=5*/f32[1536,768]{1,0:T(8,128)}), ...) | async-done | bytes 14155792 | tf_op jit(solution)/shard_map/psum | solution.py:219
  (334 shorter events, 334.3 us)
Async XLA Ops:
  7.2 253.8 %copy-start = (bf16[1536,768]{1,0:T(8,128)(2,1)S(1)}, bf16[1536,768]{1,0:T(8,128)(2,1)}, u32[]{:S(2)}) copy-start(bf16[1536,768]{1,0:T(8,128)(2,1)} %param.37) | copy-start | bytes 7077892
  7.2 247.0 %all-reduce.8.cloned.1.call-start = ((), (), s32[]{:S(2)}) async-start(), calls=%async_computation | async-start | bytes 4718592 | tf_op jit(solution)/shard_map/psum | solution.py:121
  15.0 38.0 %collective-permute-start = (bf16[768,384]{1,0:T(8,128)(2,1)}, bf16[768,384]{1,0:T(8,128)(2,1)}, u32[]{:S(2)}, u32[]{:S(2)}) collective-permute-start(bf16[768,384]{1,0:T(8,128)(2,1)} %convolution_convert_fusion.2), channel_id=1, source_target_pairs={{0,4},{2,6},{4,8},{6,10},{8,12},{10,14},{12,16},{14,18},{16,20},{1... | collective-permute-start | bytes 1769480 | tf_op jit(solution)/shard_map/ppermute | solution.py:13
  20.8 36.2 %collective-permute-start.1 = (bf16[768,384]{1,0:T(8,128)(2,1)}, bf16[768,384]{1,0:T(8,128)(2,1)}, u32[]{:S(2)}, u32[]{:S(2)}) collective-permute-start(bf16[768,384]{1,0:T(8,128)(2,1)} %convolution_convert_fusion.2), channel_id=1, source_target_pairs={{0,2},{2,4},{4,6},{6,8},{8,10},{10,12},{12,14},{14,16},{16,18},{18... | collective-permute-start | bytes 1769480 | tf_op jit(solution)/shard_map/ppermute | solution.py:13
  23.1 39.1 %collective-permute-start.2 = (bf16[768,384]{1,0:T(8,128)(2,1)}, bf16[768,384]{1,0:T(8,128)(2,1)}, u32[]{:S(2)}, u32[]{:S(2)}) collective-permute-start(bf16[768,384]{1,0:T(8,128)(2,1)} %convolution_convert_fusion.2), channel_id=1, source_target_pairs={{2,0},{4,2},{6,4},{8,6},{10,8},{12,10},{14,12},{16,14},{18,16},{20... | collective-permute-start | bytes 1769480 | tf_op jit(solution)/shard_map/ppermute | solution.py:13
  24.4 41.2 %collective-permute-start.3 = (bf16[768,384]{1,0:T(8,128)(2,1)}, bf16[768,384]{1,0:T(8,128)(2,1)}, u32[]{:S(2)}, u32[]{:S(2)}) collective-permute-start(bf16[768,384]{1,0:T(8,128)(2,1)} %convolution_convert_fusion.2), channel_id=1, source_target_pairs={{4,0},{6,2},{8,4},{10,6},{12,8},{14,10},{16,12},{18,14},{20,16},{2... | collective-permute-start | bytes 1769480 | tf_op jit(solution)/shard_map/ppermute | solution.py:13
  27.3 51.2 %collective-permute-start.4 = (bf16[768,384]{1,0:T(8,128)(2,1)}, bf16[768,384]{1,0:T(8,128)(2,1)}, u32[]{:S(2)}, u32[]{:S(2)}) collective-permute-start(bf16[768,384]{1,0:T(8,128)(2,1)} %fusion.70), channel_id=1, source_target_pairs={{0,4},{2,6},{4,8},{6,10},{8,12},{10,14},{12,16},{14,18},{16,20},{1... | collective-permute-start | bytes 1769480 | tf_op jit(solution)/shard_map/ppermute | solution.py:13
  53.0 27.5 %collective-permute-start.5 = (bf16[768,384]{1,0:T(8,128)(2,1)}, bf16[768,384]{1,0:T(8,128)(2,1)}, u32[]{:S(2)}, u32[]{:S(2)}) collective-permute-start(bf16[768,384]{1,0:T(8,128)(2,1)} %fusion.70), channel_id=1, source_target_pairs={{0,2},{2,4},{4,6},{6,8},{8,10},{10,12},{12,14},{14,16},{16,18},{18... | collective-permute-start | bytes 1769480 | tf_op jit(solution)/shard_map/ppermute | solution.py:13
  57.0 27.4 %collective-permute-start.6 = (bf16[768,384]{1,0:T(8,128)(2,1)}, bf16[768,384]{1,0:T(8,128)(2,1)}, u32[]{:S(2)}, u32[]{:S(2)}) collective-permute-start(bf16[768,384]{1,0:T(8,128)(2,1)} %fusion.70), channel_id=1, source_target_pairs={{2,0},{4,2},{6,4},{8,6},{10,8},{12,10},{14,12},{16,14},{18,16},{20... | collective-permute-start | bytes 1769480 | tf_op jit(solution)/shard_map/ppermute | solution.py:13
  62.2 26.3 %collective-permute-start.7 = (bf16[768,384]{1,0:T(8,128)(2,1)}, bf16[768,384]{1,0:T(8,128)(2,1)}, u32[]{:S(2)}, u32[]{:S(2)}) collective-permute-start(bf16[768,384]{1,0:T(8,128)(2,1)} %fusion.70), channel_id=1, source_target_pairs={{4,0},{6,2},{8,4},{10,6},{12,8},{14,10},{16,12},{18,14},{20,16},{2... | collective-permute-start | bytes 1769480 | tf_op jit(solution)/shard_map/ppermute | solution.py:13
  170.8 178.1 %all-reduce.10.cloned.1.call-start = ((), (), s32[]{:S(2)}) async-start(), calls=%async_computation.1 | async-start | bytes 4718592 | tf_op jit(solution)/shard_map/psum | solution.py:141
  173.1 179.8 %copy-start.45 = (f32[768]{0:T(1024)}, f32[768]{0:T(1024)S(1)}, u32[]{:S(2)}) copy-start(f32[768]{0:T(1024)S(1)} %convert_element_type.175) | copy-start | bytes 9220
  256.3 96.6 %copy-start.41 = (f32[768]{0:T(1024)}, f32[768]{0:T(1024)S(1)}, u32[]{:S(2)}) copy-start(f32[768]{0:T(1024)S(1)} %broadcast_multiply_fusion) | copy-start | bytes 9220
  280.2 374.0 %all-reduce.14.cloned.1.call-start = ((), (), s32[]{:S(2)}) async-start(), calls=%async_computation.3 | async-start | bytes 4718592 | tf_op jit(solution)/shard_map/psum | solution.py:130
  495.1 98.6 %copy-start.14 = (bf16[6,768,64]{1,2,0:T(8,128)(2,1)}, bf16[6,768,64]{1,2,0:T(8,128)(2,1)S(1)}, u32[]{:S(2)}) copy-start(bf16[6,768,64]{1,2,0:T(8,128)(2,1)S(1)} %get-tuple-element.111) | copy-start | bytes 1769476
  502.0 36.1 %collective-permute-start.11 = (bf16[768,384]{0,1:T(8,128)(2,1)S(1)}, bf16[768,384]{0,1:T(8,128)(2,1)S(1)}, u32[]{:S(2)}, u32[]{:S(2)}) collective-permute-start(bf16[768,384]{0,1:T(8,128)(2,1)S(1)} %bitcast.188), channel_id=1, source_target_pairs={{0,4},{2,6},{4,8},{6,10},{8,12},{10,14},{12,16},{14,18},{16,20},{1... | collective-permute-start | bytes 1769480 | tf_op jit(solution)/shard_map/ppermute | solution.py:13
  505.5 34.0 %collective-permute-start.10 = (bf16[768,384]{0,1:T(8,128)(2,1)S(1)}, bf16[768,384]{0,1:T(8,128)(2,1)S(1)}, u32[]{:S(2)}, u32[]{:S(2)}) collective-permute-start(bf16[768,384]{0,1:T(8,128)(2,1)S(1)} %bitcast.187), channel_id=1, source_target_pairs={{0,2},{2,4},{4,6},{6,8},{8,10},{10,12},{12,14},{14,16},{16,18},{18... | collective-permute-start | bytes 1769480 | tf_op jit(solution)/shard_map/ppermute | solution.py:13
  507.0 33.8 %collective-permute-start.9 = (bf16[768,384]{0,1:T(8,128)(2,1)S(1)}, bf16[768,384]{0,1:T(8,128)(2,1)S(1)}, u32[]{:S(2)}, u32[]{:S(2)}) collective-permute-start(bf16[768,384]{0,1:T(8,128)(2,1)S(1)} %bitcast.185), channel_id=1, source_target_pairs={{2,0},{4,2},{6,4},{8,6},{10,8},{12,10},{14,12},{16,14},{18,16},{20... | collective-permute-start | bytes 1769480 | tf_op jit(solution)/shard_map/ppermute | solution.py:13
  508.3 34.0 %collective-permute-start.8 = (bf16[768,384]{0,1:T(8,128)(2,1)S(1)}, bf16[768,384]{0,1:T(8,128)(2,1)S(1)}, u32[]{:S(2)}, u32[]{:S(2)}) collective-permute-start(bf16[768,384]{0,1:T(8,128)(2,1)S(1)} %bitcast.181), channel_id=1, source_target_pairs={{4,0},{6,2},{8,4},{10,6},{12,8},{14,10},{16,12},{18,14},{20,16},{2... | collective-permute-start | bytes 1769480 | tf_op jit(solution)/shard_map/ppermute | solution.py:13
  509.9 47.2 %collective-permute-start.15 = (bf16[768,384]{0,1:T(8,128)(2,1)S(1)}, bf16[768,384]{0,1:T(8,128)(2,1)S(1)}, u32[]{:S(2)}, u32[]{:S(2)}) collective-permute-start(bf16[768,384]{0,1:T(8,128)(2,1)S(1)} %bitcast.186), channel_id=1, source_target_pairs={{0,4},{2,6},{4,8},{6,10},{8,12},{10,14},{12,16},{14,18},{16,20},{1... | collective-permute-start | bytes 1769480 | tf_op jit(solution)/shard_map/ppermute | solution.py:13
  538.1 19.0 %collective-permute-start.14 = (bf16[768,384]{0,1:T(8,128)(2,1)S(1)}, bf16[768,384]{0,1:T(8,128)(2,1)S(1)}, u32[]{:S(2)}, u32[]{:S(2)}) collective-permute-start(bf16[768,384]{0,1:T(8,128)(2,1)S(1)} %bitcast.184), channel_id=1, source_target_pairs={{0,2},{2,4},{4,6},{6,8},{8,10},{10,12},{12,14},{14,16},{16,18},{18... | collective-permute-start | bytes 1769480 | tf_op jit(solution)/shard_map/ppermute | solution.py:13
  539.4 18.8 %collective-permute-start.13 = (bf16[768,384]{0,1:T(8,128)(2,1)S(1)}, bf16[768,384]{0,1:T(8,128)(2,1)S(1)}, u32[]{:S(2)}, u32[]{:S(2)}) collective-permute-start(bf16[768,384]{0,1:T(8,128)(2,1)S(1)} %bitcast.183), channel_id=1, source_target_pairs={{2,0},{4,2},{6,4},{8,6},{10,8},{12,10},{14,12},{16,14},{18,16},{20... | collective-permute-start | bytes 1769480 | tf_op jit(solution)/shard_map/ppermute | solution.py:13
  540.7 38.9 %collective-permute-start.12 = (bf16[768,384]{0,1:T(8,128)(2,1)S(1)}, bf16[768,384]{0,1:T(8,128)(2,1)S(1)}, u32[]{:S(2)}, u32[]{:S(2)}) collective-permute-start(bf16[768,384]{0,1:T(8,128)(2,1)S(1)} %bitcast.182), channel_id=1, source_target_pairs={{4,0},{6,2},{8,4},{10,6},{12,8},{14,10},{16,12},{18,14},{20,16},{2... | collective-permute-start | bytes 1769480 | tf_op jit(solution)/shard_map/ppermute | solution.py:13
  582.7 339.4 %all-reduce.12.cloned.1.call-start = ((), (), s32[]{:S(2)}) async-start(), calls=%async_computation.2 | async-start | bytes 28311552 | tf_op jit(solution)/shard_map/psum | solution.py:219
  (67 other events, 796.6 us)
Sparse Core Ops, SparseCore 0:
  171.0 83.2 all-reduce.7
  280.3 68.6 all-reduce.9
  582.8 71.3 all-reduce.13
  661.1 260.8 all-reduce.11
where the time goes:
time: 948 us; the launch traced here: 941 us
  waiting for transfers between devices  447 us (47%)
  matrix products  208 us (22%)
  other arithmetic  82.8 us (9%)
  local copies, waits for them, and re-layouts  81.6 us (9%)
  blocking collectives  65.9 us (7%)
  starting transfers between devices  40.5 us (4%)
  between operations  14.8 us (2%)
    psum x1, waiting for transfers between devices, on_device(): lax.psum((w_query_grad, query_bias_grad, w_key_grad, w_value_grad, value_...  192 us
    dot_general x24, matrix products, contract_cols(): lax.dot_general(left, right, (((1,), (1,)), ((), ())), preferred_element_...  88.8 us
    psum x1, waiting for transfers between devices, on_device(): lax.psum(matmul(attn_mixed, w_out), 'tensor') + out_bias.astype(jnp.float32)  80.5 us
    dot_general x18, matrix products, matmul(): return jnp.dot(left, right, preferred_element_type=jnp.float32)  69.8 us
    ppermute x16, waiting for transfers between devices, from_behind(): return lax.ppermute(block, axis, route)  66.4 us
    psum x1, blocking collectives, on_device(): lax.psum((w_query_grad, query_bias_grad, w_key_grad, w_value_grad, value_...  65.9 us
    psum x1, waiting for transfers between devices, on_device(): mlp_in_grad = lax.psum(contract_cols(pre_grad, w_fc1), 'tensor')  59.4 us
    dot_general x18, matrix products, contract_rows(): lax.dot_general(left, right, (((0,), (0,)), ((), ())), preferred_element_...  49.8 us
  transfers between devices with their start and end apart: 20, of which 10 were waited for; matrix products, arithmetic and copies ran while one was open for 9% of the time, Pallas kernels for 0%

commit v1 on v0

v1 whole, which is shorter than its diff:
```python
import functools

import jax
import jax.numpy as jnp
from jax import lax
from jax.experimental import pallas as pl
from jax.experimental.pallas import tpu as pltpu
from jax.sharding import PartitionSpec as P

HEAD_DIM = 64
REACH = 2
TILE = 256
PIECES = 3
NEG = -1e30
BF = jnp.bfloat16
F32 = jnp.float32
MESH = pl.DeviceIdType.MESH
VMEM = pltpu.VMEM
VMEM_BYTES = 66_000_000
DMA = pltpu.SemaphoreType.DMA


def dot_nn(left, right):
    return jnp.dot(left, right, preferred_element_type=F32)


def dot_tn(left, right):
    return lax.dot_general(left, right, (((0,), (0,)), ((), ())), preferred_element_type=F32)


def dot_nt(left, right):
    return lax.dot_general(left, right, (((1,), (1,)), ((), ())), preferred_element_type=F32)


def whole():
    return pl.BlockSpec(memory_space=VMEM)


def remote(src, dst, send_sem, recv_sem, device):
    return pltpu.make_async_remote_copy(
        src_ref=src,
        dst_ref=dst,
        send_sem=send_sem,
        recv_sem=recv_sem,
        device_id=device,
        device_id_type=MESH,
    )


def place():
    d = lax.axis_index("dp")
    chip = d // 2
    core = d - 2 * chip
    has_left = chip > 0
    has_right = chip < lax.axis_size("dp") // 2 - 1
    return d, core, has_left, has_right


def greet(targets):
    barrier = pltpu.get_barrier_semaphore()
    count = 0
    for present, device in targets:
        if present is None:
            pl.semaphore_signal(barrier, inc=1, device_id=device, device_id_type=MESH)
            count = count + 1
        else:

            @pl.when(present)
            def _():
                pl.semaphore_signal(barrier, inc=1, device_id=device, device_id_type=MESH)

            count = count + present.astype(jnp.int32)
    pl.semaphore_wait(barrier, count)


def norm_rows(values):
    middle = jnp.mean(values, axis=-1, keepdims=True)
    centred = values - middle
    spread = jnp.mean(centred * centred, axis=-1, keepdims=True)
    return centred * lax.rsqrt(spread + 1e-05)


def halo_kernel(
    x_ref, wo_ref, gain_ref, shift_ref, wq_ref, wk_ref, wv_ref, qb_ref, vb_ref,
    q_ref, k_ref, v_ref, a_ref, wof_ref,
    win, sx, rx, sy, ry, ss, rs, sf, rf, sw, rw, sv, rv,
):
    d, core, has_left, has_right = place()
    t = lax.axis_index("tensor")
    height = x_ref.shape[0]
    half = height // 2
    piece = half // PIECES
    sibling = {"dp": d + 1 - 2 * core}
    across = {"tensor": 1 - t}
    exists = (has_left, has_right)
    slots = (0, 2 * REACH)
    greet([(None, sibling), (None, across), (has_left, {"dp": d - 2}), (has_right, {"dp": d + 2})])

    def rows(which, p):
        return pl.ds(pl.multiple_of(which * half + p * piece, piece), piece)

    def x_copy(side, p):
        return remote(
            x_ref.at[rows(t, p)], win.at[slots[side], rows(t, p)], sx.at[side, p], rx.at[side, p],
            {"dp": d + 2 if side == 0 else d - 2},
        )

    def y_copy(side, p):
        spot = win.at[slots[side], rows(t, p)]
        return remote(spot, spot, sy.at[side, p], ry.at[side, p], across)

    def f_copy(which, p):
        span = rows(t if which == 0 else 1 - t, p)
        return remote(
            win.at[4 - 4 * core, span], win.at[3 - 2 * core, span], sf.at[which, p], rf.at[which, p],
            sibling,
        )

    own_copy = remote(x_ref, win.at[1 + 2 * core], ss, rs, sibling)
    part = wo_ref.shape[0] // 2
    wo_rows = pl.ds(pl.multiple_of(core * part, part), part)

    def full_rows(which):
        return pl.ds(pl.multiple_of((2 * which + core) * part, part), part)

    w_copy = remote(wo_ref.at[wo_rows], wof_ref.at[full_rows(t)], sw, rw, across)
    wf_copy = remote(wof_ref.at[full_rows(1 - t)], wof_ref.at[full_rows(1 - t)], sv, rv, sibling)

    for p in range(PIECES):
        for side in (0, 1):

            @pl.when(exists[1 - side])
            def _():
                x_copy(side, p).start()

    own_copy.start()
    gain, shift = gain_ref[...].astype(F32), shift_ref[...].astype(F32)
    query_bias, value_bias = qb_ref[...].astype(F32), vb_ref[...].astype(F32)

    def project(values, slot, start, keep=False):
        attn = (norm_rows(values.astype(F32)) * gain + shift).astype(BF)
        out = pl.ds(pl.multiple_of(slot * height + start, 128), half)
        if keep:
            a_ref[pl.ds(pl.multiple_of(start, half), half), :] = attn
        q_ref[out, :] = ((dot_nn(attn, wq_ref[...]) + query_bias) * HEAD_DIM**-0.5).astype(BF)
        k_ref[out, :] = dot_nn(attn, wk_ref[...]).astype(BF)
        v_ref[out, :] = (dot_nn(attn, wv_ref[...]) + value_bias).astype(BF)

    def project_half(slot, which):
        start = which * half
        project(win[slot, pl.ds(pl.multiple_of(start, half), half), :], slot, start)

    def project_block(slot):
        def step(i, carry):
            project_half(slot, i)
            return carry

        lax.fori_loop(0, 2, step, 0)

    def own_step(i, carry):
        project(x_ref[pl.ds(pl.multiple_of(i * half, half), half), :], REACH, i * half, True)
        return carry

    def pass_on(p):
        for side in (0, 1):

            @pl.when(exists[side])
            def _():
                x_copy(side, p).wait_recv()
                y_copy(side, p).start()

            @pl.when(jnp.logical_and(exists[side], core == 1 - side))
            def _():
                f_copy(0, p).start()

    lax.fori_loop(0, 2, own_step, 0)
    wof_ref[pl.ds(pl.multiple_of(t * 2 * part, part), 2 * part), :] = wo_ref[...]
    pass_on(0)
    own_copy.wait_recv()
    project_block(3 - 2 * core)
    for p in range(1, PIECES):
        pass_on(p)
    w_copy.start()
    for side in (0, 1):

        @pl.when(exists[side])
        def _():
            project_half(slots[side], t)

    for p in range(PIECES):
        for side in (0, 1):

            @pl.when(exists[side])
            def _():
                y_copy(side, p).wait_recv()

            @pl.when(jnp.logical_and(exists[side], core == 1 - side))
            def _():
                f_copy(1, p).start()

    w_copy.wait_recv()
    wf_copy.start()
    for side in (0, 1):

        @pl.when(exists[side])
        def _():
            project_half(slots[side], 1 - t)

        @pl.when(jnp.logical_and(exists[side], core == side))
        def _():
            for which in (0, 1):
                for p in range(PIECES):
                    f_copy(which, p).wait_recv()
            project_block(1 + 2 * core)

    wf_copy.wait_recv()
    for copy in (own_copy, w_copy, wf_copy):
        copy.wait_send()
    for p in range(PIECES):
        for side in (0, 1):

            @pl.when(exists[1 - side])
            def _():
                x_copy(side, p).wait_send()

            @pl.when(exists[side])
            def _():
                y_copy(side, p).wait_send()

            @pl.when(jnp.logical_and(exists[side], core == 1 - side))
            def _():
                f_copy(0, p).wait_send()
                f_copy(1, p).wait_send()


def halo_qkv(x, wo, gain, shift, wq, wk, wv, qb, vb):
    height, width = x.shape
    cols = wq.shape[1]
    blocks = 2 * REACH + 1
    wide = jax.ShapeDtypeStruct((blocks * height, cols), BF)
    pair = DMA((2, PIECES))
    return pl.pallas_call(
        halo_kernel,
        out_shape=(
            wide, wide, wide,
            jax.ShapeDtypeStruct((height, width), BF),
            jax.ShapeDtypeStruct((2 * wo.shape[0], wo.shape[1]), BF),
        ),
        in_specs=[whole()] * 9,
        out_specs=[whole()] * 5,
        scratch_shapes=[pltpu.VMEM((blocks, height, width), BF)]
        + [pair, pair, pair, pair, DMA, DMA, pair, pair, DMA, DMA, DMA, DMA],
        compiler_params=pltpu.CompilerParams(
            collective_id=0, has_side_effects=True, vmem_limit_bytes=VMEM_BYTES
        ),
        name="halo_qkv",
    )(x, wo, gain, shift, wq, wk, wv, qb, vb)


def back_halo_kernel(x_ref, st_ref, xw_ref, sw_ref, sx, rx, ss, rs, sf, rf):
    d, core, has_left, has_right = place()
    height = x_ref.shape[0]
    piece = height // PIECES
    sibling = {"dp": d + 1 - 2 * core}
    exists = (has_left, has_right)
    slots = (0, 2 * REACH)
    greet([(None, sibling), (has_left, {"dp": d - 2}), (has_right, {"dp": d + 2})])

    def refs(p):
        if p == PIECES:
            return st_ref, lambda slot: sw_ref.at[slot]
        span = pl.ds(p * piece, piece)
        return x_ref.at[span], lambda slot: xw_ref.at[slot, span]

    def x_copy(side, p):
        src, dst = refs(p)
        return remote(
            src, dst(slots[side]), sx.at[side, p], rx.at[side, p],
            {"dp": d + 2 if side == 0 else d - 2},
        )

    def s_copy(p):
        src, dst = refs(p)
        return remote(src, dst(1 + 2 * core), ss.at[p], rs.at[p], sibling)

    def f_copy(p):
        _, dst = refs(p)
        return remote(dst(4 - 4 * core), dst(3 - 2 * core), sf.at[p], rf.at[p], sibling)

    order = (PIECES,) + tuple(range(PIECES))
    for p in order:
        for side in (0, 1):

            @pl.when(exists[1 - side])
            def _():
                x_copy(side, p).start()

    for p in order:
        s_copy(p).start()
    xw_ref[REACH] = x_ref[...]
    sw_ref[REACH] = st_ref[...]
    for p in order:
        for side in (0, 1):

            @pl.when(exists[side])
            def _():
                x_copy(side, p).wait_recv()

            @pl.when(jnp.logical_and(exists[side], core == 1 - side))
            def _():
                f_copy(p).start()

    for p in order:
        s_copy(p).wait()
        for side in (0, 1):

            @pl.when(exists[1 - side])
            def _():
                x_copy(side, p).wait_send()

            @pl.when(jnp.logical_and(exists[side], core == 1 - side))
            def _():
                f_copy(p).wait_send()

            @pl.when(jnp.logical_and(exists[side], core == side))
            def _():
                f_copy(p).wait_recv()


def back_halo(x, stats):
    blocks = 2 * REACH + 1
    pair, line = DMA((2, PIECES + 1)), DMA((PIECES + 1,))
    return pl.pallas_call(
        back_halo_kernel,
        out_shape=(
            jax.ShapeDtypeStruct((blocks,) + x.shape, x.dtype),
            jax.ShapeDtypeStruct((blocks,) + stats.shape, stats.dtype),
        ),
        in_specs=[whole()] * 2,
        out_specs=[whole()] * 2,
        scratch_shapes=[pair, pair, line, line, line, line],
        compiler_params=pltpu.CompilerParams(
            collective_id=1, has_side_effects=True, vmem_limit_bytes=VMEM_BYTES
        ),
        name="back_halo",
    )(x, stats)


def only(values, lower, keep_low):
    return jnp.where(lower if keep_low else jnp.logical_not(lower), values, jnp.zeros_like(values))


def low_lanes(shape):
    return lax.broadcasted_iota(jnp.int32, shape, 1) < HEAD_DIM


def key_tile(j):
    return pl.ds(pl.multiple_of(j * TILE, TILE), TILE)


def attend_kernel(b_ref, q_ref, k_ref, v_ref, own_ref, win_ref, o_ref, lse_ref, row_ref, s_ref, m_ref, l_ref, acc_ref):
    i = pl.program_id(1)
    lo, hi = b_ref[0, i], b_ref[1, i]
    lower = low_lanes((TILE, 128))
    query = q_ref[...]
    queries = (only(query, lower, True), only(query, lower, False))
    own = own_ref[...]
    m_ref[...] = jnp.full(m_ref.shape, NEG, F32)
    l_ref[...] = jnp.zeros(l_ref.shape, F32)
    acc_ref[...] = jnp.zeros(acc_ref.shape, F32)

    def score(j, carry):
        keys = k_ref[key_tile(j), :]
        same = own == win_ref[j]
        for h in (0, 1):
            s = jnp.where(same, dot_nt(queries[h], keys), NEG)
            s_ref[h, j - lo] = s
            m_ref[h] = jnp.maximum(m_ref[h], jnp.maximum(s[:, :128], s[:, 128:]))
        return carry

    lax.fori_loop(lo, hi, score, 0)
    tops = [jnp.max(m_ref[h], axis=1, keepdims=True) for h in (0, 1)]

    def weigh(j, carry):
        values = v_ref[key_tile(j), :]
        for h in (0, 1):
            e = jnp.exp(s_ref[h, j - lo] - tops[h])
            l_ref[h] += e[:, :128] + e[:, 128:]
            acc_ref[h] += dot_nn(e.astype(BF), values)
        return carry

    lax.fori_loop(lo, hi, weigh, 0)
    totals = [jnp.sum(l_ref[h], axis=1, keepdims=True) for h in (0, 1)]
    o_ref[...] = jnp.where(lower, acc_ref[0] / totals[0], acc_ref[1] / totals[1]).astype(BF)
    logs = jnp.where(lower, tops[0] + jnp.log(totals[0]), tops[1] + jnp.log(totals[1]))
    lse_ref[0] = logs
    turned = jnp.transpose(logs)
    row_ref[0, 0:8, :] = turned[0:8]
    row_ref[0, 8:16, :] = turned[HEAD_DIM : HEAD_DIM + 8]


def attend(bounds, q, k, v, own, win):
    window, cols = k.shape
    tiles = own.shape[0] // TILE
    pairs = cols // 128
    first = REACH * tiles
    most = 2 * REACH * tiles + tiles
    grid = pltpu.PrefetchScalarGridSpec(
        num_scalar_prefetch=1,
        grid=(pairs, tiles),
        in_specs=[
            pl.BlockSpec((TILE, 128), lambda p, i, b: (first + i, p)),
            pl.BlockSpec((window, 128), lambda p, i, b: (0, p)),
            pl.BlockSpec((window, 128), lambda p, i, b: (0, p)),
            pl.BlockSpec((TILE, 1), lambda p, i, b: (i, 0)),
            pl.BlockSpec(win.shape, lambda p, i, b: (0, 0, 0)),
        ],
        out_specs=[
            pl.BlockSpec((TILE, 128), lambda p, i, b: (i, p)),
            pl.BlockSpec((1, TILE, 128), lambda p, i, b: (p, i, 0)),
            pl.BlockSpec((1, 16, TILE), lambda p, i, b: (p, 0, i)),
        ],
        scratch_shapes=[
            pltpu.VMEM((2, most, TILE, TILE), F32),
            pltpu.VMEM((2, TILE, 128), F32),
            pltpu.VMEM((2, TILE, 128), F32),
            pltpu.VMEM((2, TILE, 128), F32),
        ],
    )
    return pl.pallas_call(
        attend_kernel,
        grid_spec=grid,
        out_shape=(
            jax.ShapeDtypeStruct((tiles * TILE, cols), BF),
            jax.ShapeDtypeStruct((pairs, tiles * TILE, 128), F32),
            jax.ShapeDtypeStruct((pairs, 16, tiles * TILE), F32),
        ),
        compiler_params=pltpu.CompilerParams(vmem_limit_bytes=VMEM_BYTES),
        name="attend",
    )(bounds, q, k, v, own, win)


def query_back_kernel(b_ref, q_ref, k_ref, v_ref, o_ref, g_ref, lse_ref, own_ref, win_ref, dq_ref, acc_ref):
    i = pl.program_id(1)
    lo, hi = b_ref[0, i], b_ref[1, i]
    lower = low_lanes((TILE, 128))
    query, grad = q_ref[...], g_ref[...]
    queries = (only(query, lower, True), only(query, lower, False))
    grads = (only(grad, lower, True), only(grad, lower, False))
    product = grad.astype(F32) * o_ref[...].astype(F32)
    centres = [jnp.sum(only(product, lower, h == 0), axis=1, keepdims=True) for h in (0, 1)]
    logs = [lse_ref[0, :, 0:1], lse_ref[0, :, HEAD_DIM : HEAD_DIM + 1]]
    own = own_ref[...]
    acc_ref[...] = jnp.zeros(acc_ref.shape, F32)

    def step(j, carry):
        keys, values = k_ref[key_tile(j), :], v_ref[key_tile(j), :]
        same = own == win_ref[j]
        for h in (0, 1):
            s = jnp.where(same, dot_nt(queries[h], keys), NEG)
            probs = jnp.exp(s - logs[h])
            d_score = probs * (dot_nt(grads[h], values) - centres[h])
            acc_ref[h] += dot_nn(d_score.astype(BF), keys)
        return carry

    lax.fori_loop(lo, hi, step, 0)
    dq_ref[...] = (jnp.where(lower, acc_ref[0], acc_ref[1]) * HEAD_DIM**-0.5).astype(BF)


def query_back(bounds, q, k, v, o, g, lse, own, win):
    window, cols = k.shape
    tiles = own.shape[0] // TILE
    pairs = cols // 128
    first = REACH * tiles
    tile = pl.BlockSpec((TILE, 128), lambda p, i, b: (i, p))
    grid = pltpu.PrefetchScalarGridSpec(
        num_scalar_prefetch=1,
        grid=(pairs, tiles),
        in_specs=[
            pl.BlockSpec((TILE, 128), lambda p, i, b: (first + i, p)),
            pl.BlockSpec((window, 128), lambda p, i, b: (0, p)),
            pl.BlockSpec((window, 128), lambda p, i, b: (0, p)),
            tile,
            tile,
            pl.BlockSpec((1, TILE, 128), lambda p, i, b: (p, i, 0)),
            pl.BlockSpec((TILE, 1), lambda p, i, b: (i, 0)),
            pl.BlockSpec(win.shape, lambda p, i, b: (0, 0, 0)),
        ],
        out_specs=tile,
        scratch_shapes=[pltpu.VMEM((2, TILE, 128), F32)],
    )
    return pl.pallas_call(
        query_back_kernel,
        grid_spec=grid,
        out_shape=jax.ShapeDtypeStruct((tiles * TILE, cols), BF),
        compiler_params=pltpu.CompilerParams(vmem_limit_bytes=VMEM_BYTES),
        name="query_back",
    )(bounds, q, k, v, o, g, lse, own, win)


def key_back_kernel(b_ref, q_ref, k_ref, v_ref, g_ref, st_ref, own_ref, win_ref, dk_ref, dv_ref, acck_ref, accv_ref):
    p, i = pl.program_id(0), pl.program_id(1)
    lo, hi = b_ref[0, i], b_ref[1, i]
    lower = low_lanes((TILE, 128))
    key, value = k_ref[...], v_ref[...]
    keys = (only(key, lower, True), only(key, lower, False))
    values = (only(value, lower, True), only(value, lower, False))
    own = own_ref[...]
    acck_ref[...] = jnp.zeros(acck_ref.shape, F32)
    accv_ref[...] = jnp.zeros(accv_ref.shape, F32)

    def step(j, carry):
        queries, grads = q_ref[key_tile(j), :], g_ref[key_tile(j), :]
        same = own == win_ref[j]
        for h in (0, 1):
            logs = st_ref[j, pl.ds(2 * p + h, 1), :]
            centres = st_ref[j, pl.ds(8 + 2 * p + h, 1), :]
            s = jnp.where(same, dot_nt(keys[h], queries), NEG)
            probs = jnp.exp(s - logs)
            d_score = probs * (dot_nt(values[h], grads) - centres)
            accv_ref[h] += dot_nn(probs.astype(BF), grads)
            acck_ref[h] += dot_nn(d_score.astype(BF), queries)
        return carry

    lax.fori_loop(lo, hi, step, 0)
    dk_ref[...] = jnp.where(lower, acck_ref[0], acck_ref[1]).astype(BF)
    dv_ref[...] = jnp.where(lower, accv_ref[0], accv_ref[1]).astype(BF)


def key_back(bounds, q, k, v, g, stats, own, win):
    window, cols = k.shape
    tiles = own.shape[0] // TILE
    pairs = cols // 128
    first = REACH * tiles
    tile = pl.BlockSpec((TILE, 128), lambda p, i, b: (i, p))
    centre = pl.BlockSpec((TILE, 128), lambda p, i, b: (first + i, p))
    strip = pl.BlockSpec((window, 128), lambda p, i, b: (0, p))
    grid = pltpu.PrefetchScalarGridSpec(
        num_scalar_prefetch=1,
        grid=(pairs, tiles),
        in_specs=[
            strip,
            centre,
            centre,
            strip,
            pl.BlockSpec(stats.shape, lambda p, i, b: (0, 0, 0)),
            pl.BlockSpec((TILE, 1), lambda p, i, b: (i, 0)),
            pl.BlockSpec(win.shape, lambda p, i, b: (0, 0, 0)),
        ],
        out_specs=[tile, tile],
        scratch_shapes=[pltpu.VMEM((2, TILE, 128), F32), pltpu.VMEM((2, TILE, 128), F32)],
    )
    return pl.pallas_call(
        key_back_kernel,
        grid_spec=grid,
        out_shape=(jax.ShapeDtypeStruct((tiles * TILE, cols), BF),) * 2,
        compiler_params=pltpu.CompilerParams(vmem_limit_bytes=VMEM_BYTES),
        name="key_back",
    )(bounds, q, k, v, g, stats, own, win)


def ring_kernel(arrays, *refs):
    given = refs[:arrays]
    outs = refs[arrays : 2 * arrays]
    sibs = refs[2 * arrays : 3 * arrays]
    bufs = refs[3 * arrays : 4 * arrays]
    ss, rs, sr, rr, sg, rg, sc, rc = refs[4 * arrays :]
    d = lax.axis_index("dp")
    n = lax.axis_size("dp") // 2
    chip = d // 2
    core = d - 2 * chip
    sibling = {"dp": d + 1 - 2 * core}
    odd = chip - 2 * (chip // 2)
    spot = (1 - odd) * (chip // 2) + odd * (n - 1 - chip // 2)
    here = (1 - core) * spot + core * (n - 1 - spot)

    def wrap(index):
        return lax.rem(index + 2 * n, n)

    def device_at(rank):
        walk = (1 - core) * rank + core * (n - 1 - rank)
        late = walk // (n // 2)
        return 2 * ((1 - late) * (2 * walk) + late * (2 * (n - walk) - 1)) + core

    after = {"dp": device_at(wrap(here + 1))}
    before = {"dp": device_at(wrap(here - 1))}
    greet([(None, sibling), (None, after), (None, before)])

    def spans(a, owner, j):
        rows, cols = given[a].shape[0] // 2, given[a].shape[1]
        count = cols // bufs[a].shape[2]
        high, wide = bufs[a].shape[1], bufs[a].shape[2]
        line = j // count
        row = pl.multiple_of(owner * rows + line * high, high)
        col = pl.multiple_of((j - line * count) * wide, wide)
        return pl.ds(row, high), pl.ds(col, wide)

    def s_copy(a):
        rows = given[a].shape[0] // 2
        span = pl.ds(pl.multiple_of((1 - core) * rows, rows), rows)
        return remote(given[a].at[span], sibs[a], ss.at[a], rs.at[a], sibling)

    def r_copy(a, s):
        return remote(bufs[a].at[s], bufs[a].at[s + 1], sr.at[a, s], rr.at[a, s], after)

    def g_copy(a, s):
        spot = outs[a].at[spans(a, core, wrap(here + 1 - s))]
        return remote(spot, spot, sg.at[a, s], rg.at[a, s], after)

    def c_copy(a, s):
        spot = outs[a].at[spans(a, core, wrap(here + 1 - s))]
        return remote(spot, spot, sc.at[a, s], rc.at[a, s], sibling)

    def terms(a, j):
        mine = given[a][spans(a, core, j)].astype(F32)
        return mine + sibs[a][spans(a, 0, j)].astype(F32)

    for a in range(arrays):
        s_copy(a).start()
    for a in range(arrays):
        s_copy(a).wait_recv()
        bufs[a][0] = terms(a, here).astype(bufs[a].dtype)
        r_copy(a, 0).start()

    def reduce_step(s, carry):
        for a in range(arrays):
            j = wrap(here - s)
            local = terms(a, j)
            r_copy(a, s - 1).wait_recv()
            bufs[a][s] = (bufs[a][s].astype(F32) + local).astype(bufs[a].dtype)
            r_copy(a, s).start()
        return carry

    lax.fori_loop(1, n - 1, reduce_step, 0)
    for a in range(arrays):
        j = wrap(here + 1)
        local = terms(a, j)
        r_copy(a, n - 2).wait_recv()
        done = (bufs[a][n - 1].astype(F32) + local).astype(bufs[a].dtype)
        outs[a][spans(a, core, j)] = done
        g_copy(a, 0).start()
        c_copy(a, 0).start()

    def gather_step(s, carry):
        for a in range(arrays):
            g_copy(a, s - 1).wait_recv()
            g_copy(a, s).start()
            c_copy(a, s).start()
        return carry

    lax.fori_loop(1, n - 1, gather_step, 0)
    for a in range(arrays):
        g_copy(a, n - 2).wait_recv()
        c_copy(a, n - 1).start()
    for a in range(arrays):
        s_copy(a).wait_send()
        c_copy(a, n - 1).wait()

    def settle(s, carry):
        for a in range(arrays):
            r_copy(a, s).wait_send()
            g_copy(a, s).wait_send()
            c_copy(a, s).wait()
        return carry

    lax.fori_loop(0, n - 1, settle, 0)


def ring_sum(values, ident):
    n = lax.axis_size("dp") // 2
    count = len(values)
    sibs, bufs = [], []
    for value in values:
        rows, cols = value.shape
        wide = min(cols, 384)
        sibs.append(pltpu.VMEM((rows // 2, cols), value.dtype))
        bufs.append(pltpu.VMEM((n, rows * cols // (2 * n * wide), wide), value.dtype))
    return pl.pallas_call(
        functools.partial(ring_kernel, count),
        out_shape=tuple(jax.ShapeDtypeStruct(v.shape, v.dtype) for v in values),
        in_specs=[whole()] * count,
        out_specs=[whole()] * count,
        scratch_shapes=sibs
        + bufs
        + [DMA((count,)), DMA((count,))]
        + [DMA((count, n - 1))] * 4
        + [DMA((count, n))] * 2,
        compiler_params=pltpu.CompilerParams(
            collective_id=ident, has_side_effects=True, vmem_limit_bytes=VMEM_BYTES
        ),
        name="ring_sum",
    )(*values)


def swapped(value):
    return lax.ppermute(value, "tensor", [(0, 1), (1, 0)])


def norm_back(grad, source, gain):
    middle = jnp.mean(source, axis=-1, keepdims=True)
    centred = source - middle
    inverse = lax.rsqrt(jnp.mean(centred * centred, axis=-1, keepdims=True) + 1e-05)
    n = centred * inverse
    t = grad * gain
    back = (t - jnp.mean(t, axis=-1, keepdims=True) - n * jnp.mean(t * n, axis=-1, keepdims=True)) * inverse
    return back, jnp.sum(grad * n, axis=0), jnp.sum(grad, axis=0)


def on_device(
    inputs, clip_ids, attn_gain, attn_shift, w_query, query_bias, w_key, w_value, value_bias,
    w_out, out_bias, mlp_gain, mlp_shift, w_fc1, fc1_bias, w_fc2, fc2_bias, cotangent,
):
    height, width = inputs.shape
    tiles = height // TILE
    d = lax.axis_index("dp")
    t = lax.axis_index("tensor")
    reach = REACH * height
    heads = w_query.shape[1] // HEAD_DIM

    padded = jnp.pad(clip_ids, (reach, reach), constant_values=-1)
    window = lax.dynamic_slice_in_dim(padded, d * height, height + 2 * reach)
    own = lax.dynamic_slice_in_dim(clip_ids, d * height, height)
    firsts, lasts = own[::TILE], own[TILE - 1 :: TILE]
    origin = d * height - reach
    begin = jnp.sum((clip_ids[None, :] < firsts[:, None]).astype(jnp.int32), axis=1) - origin
    end = jnp.sum((clip_ids[None, :] <= lasts[:, None]).astype(jnp.int32), axis=1) - origin
    bounds = jnp.stack([begin // TILE, (end + TILE - 1) // TILE])
    own = own[:, None]
    window = window.reshape(-1, 1, TILE)

    row = lambda v: v[None, :]
    q, k, v, attn_input, w_out_full = halo_qkv(
        inputs, w_out, row(attn_gain), row(attn_shift), w_query, w_key, w_value,
        row(query_bias), row(value_bias),
    )
    mixed, lse, lse_rows = attend(bounds, q, k, v, own, window)
    other = swapped(mixed)
    flip = t == 0
    w_mine = w_out
    w_other = lax.dynamic_slice_in_dim(w_out_full, (1 - t) * w_out.shape[0], w_out.shape[0])
    source = inputs.astype(F32)
    residual = source + dot_nn(mixed, w_mine) + dot_nn(other, w_other) + out_bias.astype(F32)
    mlp_input = (norm_rows(residual) * mlp_gain.astype(F32) + mlp_shift.astype(F32)).astype(BF)
    preact = dot_nn(mlp_input, w_fc1) + fc1_bias.astype(F32)
    cdf = 0.5 * (1.0 + lax.erf(preact * (2.0**-0.5)))
    pdf = jnp.exp(-0.5 * preact * preact) * 0.3989422804014327
    activated = (preact * cdf).astype(BF)
    slope = cdf + preact * pdf
    pre_grad = (dot_nt(cotangent, w_fc2) * slope).astype(BF)
    part = dot_nt(pre_grad, w_fc1).astype(BF)
    mlp_in_grad = part.astype(F32) + swapped(part).astype(F32)
    out_part = dot_nn(activated, w_fc2).astype(BF)
    layer_out = (
        residual + (out_part.astype(F32) + swapped(out_part).astype(F32)) + fc2_bias.astype(F32)
    ).astype(BF)
    cot = cotangent.astype(F32)
    resid_back, mlp_gain_grad, mlp_shift_grad = norm_back(mlp_in_grad, residual, mlp_gain.astype(F32))
    residual_grad = cot + resid_back
    attn_grad_low = residual_grad.astype(BF)
    mixed_grad = dot_nt(attn_grad_low, w_out).astype(BF)

    fc1_grad = dot_tn(mlp_input, pre_grad).astype(BF)
    fc2_grad = dot_tn(activated, cotangent).astype(BF)
    out_grad = dot_tn(attn_grad_low, mixed).astype(BF)
    fc2_bias_grad = jnp.sum(cot, axis=0)
    fc1_bias_grad = jnp.sum(pre_grad.astype(F32), axis=0)
    out_bias_grad = jnp.sum(attn_grad_low.astype(F32), axis=0)

    product = (mixed_grad.astype(F32) * mixed.astype(F32)).reshape(height, heads, HEAD_DIM)
    centres = jnp.sum(product, axis=2).T
    logs = jnp.stack([lse_rows[h // 2, 8 * (h % 2)] for h in range(heads)])
    gap = jnp.zeros((8 - heads, height), F32)
    stats = jnp.concatenate([logs, gap, centres, gap])
    grad_win, stat_win = back_halo(mixed_grad, stats)
    grad_win = grad_win.reshape(-1, grad_win.shape[2])
    stat_win = stat_win.reshape(-1, 16, tiles, TILE).transpose(0, 2, 1, 3).reshape(-1, 16, TILE)
    query_low = query_back(bounds, q, k, v, mixed, mixed_grad, lse, own, window)
    key_low, value_low = key_back(bounds, q, k, v, grad_win, stat_win, own, window)

    attn_part = (
        dot_nt(query_low, w_query) + dot_nt(key_low, w_key) + dot_nt(value_low, w_value)
    ).astype(BF)
    attn_in_grad = attn_part.astype(F32) + swapped(attn_part).astype(F32)
    source_back, attn_gain_grad, attn_shift_grad = norm_back(attn_in_grad, source, attn_gain.astype(F32))
    inputs_grad = residual_grad + source_back
    query_bias_grad = jnp.sum(query_low.astype(F32), axis=0)
    value_bias_grad = jnp.sum(value_low.astype(F32), axis=0)
    attn_weights = jnp.concatenate(
        [
            dot_tn(attn_input, query_low).astype(BF),
            dot_tn(attn_input, key_low).astype(BF),
            dot_tn(attn_input, value_low).astype(BF),
            out_grad,
        ],
        axis=1,
    )
    vectors = [
        query_bias_grad, value_bias_grad, out_bias_grad, attn_gain_grad, attn_shift_grad,
        fc1_bias_grad, fc2_bias_grad, mlp_gain_grad, mlp_shift_grad,
    ]
    sizes = [vector.shape[0] for vector in vectors]
    room = lax.axis_size("dp") * 1024
    packed = jnp.pad(jnp.concatenate(vectors), (0, room - sum(sizes))).reshape(-1, 128)
    attn_sum, fc1_sum, fc2_sum, packed_sum = ring_sum([attn_weights, fc1_grad, fc2_grad, packed], 2)
    flat = packed_sum.reshape(-1)
    sums, start = [], 0
    for size in sizes:
        sums.append(flat[start : start + size])
        start += size
    (
        query_bias_grad, value_bias_grad, out_bias_grad, attn_gain_grad, attn_shift_grad,
        fc1_bias_grad, fc2_bias_grad, mlp_gain_grad, mlp_shift_grad,
    ) = sums
    cols = w_query.shape[1]
    pieces = [attn_sum[:, i * cols : (i + 1) * cols].astype(F32) for i in range(4)]
    return (
        layer_out, inputs_grad, attn_gain_grad, attn_shift_grad,
        pieces[0], query_bias_grad, pieces[1], pieces[2], value_bias_grad,
        pieces[3].T, out_bias_grad, mlp_gain_grad, mlp_shift_grad,
        fc1_sum.astype(F32), fc1_bias_grad, fc2_sum.astype(F32), fc2_bias_grad,
    )


def solution(mesh):
    rows, cols, split, every = P("dp", None), P(None, "tensor"), P("tensor"), P()
    tall = P("tensor", None)
    in_specs = (
        rows, every, every, every, cols, split, cols, cols, split, tall, every, every, every,
        cols, split, tall, every, rows,
    )
    out_specs = (
        rows, rows, every, every, cols, split, cols, cols, split, tall, every, every, every,
        cols, split, tall, every,
    )
    return jax.shard_map(on_device, mesh=mesh, in_specs=in_specs, out_specs=out_specs, check_vma=False)
```

time: 948 us -> 470 us (0.50)
  waiting for transfers between devices: 447 us -> 63.6 us
  Pallas kernels: 0 us -> 302 us
  matrix products: 208 us -> 35.4 us
  blocking collectives: 65.9 us -> 0 us
  other arithmetic: 82.8 us -> 29.1 us
  local copies, waits for them, and re-layouts: 81.6 us -> 28.8 us
  starting transfers between devices: 40.5 us -> 3.29 us
  between operations: 14.8 us -> 1.81 us
    psum x4 -> x0, waiting for transfers between devices: 380 us -> none  [the longest x1 192 us: on_device(): lax.psum((w_query_grad, query_bias_grad, w_key_grad, w_value_grad, value_...]
    pallas_call x0 -> x6, Pallas kernels: none -> 302 us  [the longest x1 111 us: ring_sum(): pl.pallas_call(functools.partial(ring_kernel, count), out_shape=tuple((ja...]
    dot_general x60 -> x16, matrix products: 208 us -> 35.4 us  [the longest x6 15 us: dot_nt(): lax.dot_general(left, right, (((1,), (1,)), ((), ())), preferred_element_...]
    psum x1 -> x0, blocking collectives: 65.9 us -> none  [on_device(): lax.psum((w_query_grad, query_bias_grad, w_key_grad, w_value_grad, value_...]
    ppermute x16 -> x4, starting transfers between devices: 40.1 us -> 3.29 us  [swapped(): return lax.ppermute(value, 'tensor', [(0, 1), (1, 0)])]
    unnamed x146 -> x109, local copies, waits for them, and re-layouts: 46.8 us -> 11.7 us
    convert_element_type x19 -> x8, other arithmetic: 38 us -> 7.77 us  [the longest x1 2.83 us: on_device(): fc1_sum.astype(F32)]
    reduce_sum x18 -> x10, other arithmetic: 32.8 us -> 11.2 us  [the longest x1 3.57 us: on_device(): out_bias_grad = jnp.sum(attn_grad_low.astype(F32), axis=0)]
  transfers between devices with their start and end apart: 20 -> 4, of which waited for: 10 -> 4; matrix products, arithmetic and copies ran while one was open for 9% -> 5% of each run, Pallas kernels for 0% -> 0%
where the time goes in v1:
time: 470 us; the launch traced here: 464 us
  Pallas kernels  302 us (64%)
  waiting for transfers between devices  63.6 us (14%)
  matrix products  35.4 us (8%)
  other arithmetic  29.1 us (6%)
  local copies, waits for them, and re-layouts  28.8 us (6%)
    pallas_call x1, Pallas kernels, ring_sum(): pl.pallas_call(functools.partial(ring_kernel, count), out_shape=tuple((ja...  111 us
    pallas_call x1, Pallas kernels, back_halo(): pl.pallas_call(back_halo_kernel, out_shape=(jax.ShapeDtypeStruct((blocks,...  83.1 us
    ppermute x4, waiting for transfers between devices, swapped(): return lax.ppermute(value, 'tensor', [(0, 1), (1, 0)])  63.6 us
    pallas_call x1, Pallas kernels, halo_qkv(): pl.pallas_call(halo_kernel, out_shape=(wide, wide, wide, jax.ShapeDtypeSt...  38.2 us
    pallas_call x1, Pallas kernels, key_back(): pl.pallas_call(key_back_kernel, grid_spec=grid, out_shape=(jax.ShapeDtype...  24.1 us
    pallas_call x1, Pallas kernels, query_back(): pl.pallas_call(query_back_kernel, grid_spec=grid, out_shape=jax.ShapeDtyp...  24 us
    pallas_call x1, Pallas kernels, attend(): pl.pallas_call(attend_kernel, grid_spec=grid, out_shape=(jax.ShapeDtypeSt...  22.1 us
    dot_general x6, matrix products, dot_nt(): lax.dot_general(left, right, (((1,), (1,)), ((), ())), preferred_element_...  15 us
  transfers between devices with their start and end apart: 4, of which 4 were waited for; matrix products, arithmetic and copies ran while one was open for 5% of the time, Pallas kernels for 0%

profile of v1, /device:TPU:0, one launch (start us, length us, event | category | flops | bytes accessed | tf_op | source)
XLA Modules:
  0.0 464.2 jit_solution(14303656903441758063)
XLA Ops:
  10.7 38.2 %halo_qkv.1 = (bf16[3840,384]{1,0:T(8,128)(2,1)}, bf16[3840,384]{1,0:T(8,128)(2,1)}, bf16[3840,384]{1,0:T(8,128)(2,1)}, bf16[768,768]{1,0:T(8,128)(2,1)}, bf16[768,768]{1,0:T(8,128)(2,1)}) custom-call(bf16[768,768]{1,0:T(8,128)(2,1)} %x_ref.1, bf16[384,768]{1,0:T(8,128)(2,1)} %wo_ref.1, bf16[1,768]{1,0:T(2,128)(2,1)} %broadcast_in_dim.12.gain_ref, ...), custom_call_target="tpu_custom_call" | custom-call | tf_op jit(solution)/shard_map/halo_qkv/pallas_call | solution.py:242
  48.9 22.1 %attend.1 = (bf16[768,384]{1,0:T(8,128)(2,1)}, f32[3,768,128]{2,1,0:T(8,128)}, f32[3,16,768]{2,1,0:T(8,128)}) custom-call(s32[2,3]{1,0:T(2,128)} %pad_add_fusion.b_ref, bf16[3840,384]{1,0:T(8,128)(2,1)} %get-tuple-element.33.q_ref, bf16[3840,384]{1,0:T(8,128)(2,1)} %get-tuple-element.34.k_ref, bf16[3840,384]{1,0:T(8,128)(2,1)} %get-tuple-element.35.v_ref, ...), custom_call_target="tpu_custom_call" | custom-call | tf_op jit(solution)/shard_map/attend/pallas_call | solution.py:430
  80.3 3.8 collective-permute-done
  84.1 2.1 fusion.31
  87.9 2.9 multiply_convert_fusion
  90.8 4.9 %convert_reduce_fusion = (f32[1536]{0:T(1024)}, bf16[768,1536]{1,0:T(8,128)(2,1)S(1)}) fusion(f32[768,1536]{1,0:T(8,128)S(1)} %get-tuple-element.138, f32[1536]{0:T(1024)S(1)} %copy-done.37, bf16[768,768]{1,0:T(8,128)(2,1)S(1)} %copy-done.19, bf16[1536,768]{1,0:T(8,128)(2,1)S(1)} %copy-done.46), kind=kOutput, calls=%fused_computation.7 | convolution fusion | flops 1827273216 | bytes 10629120 | tf_op jit(solution)/shard_map/dot_general | solution.py:32
  98.3 2.1 convolution_convert_fusion.3
  102.1 3.5 convolution_convert_fusion.1.refs_1_
  105.6 3.6 convolution_convert_fusion.refs_2_
  109.2 15.0 %collective-permute-done.2 = bf16[768,768]{0,1:T(8,128)(2,1)S(1)} collective-permute-done((bf16[768,768]{0,1:T(8,128)(2,1)S(1)}, bf16[768,768]{0,1:T(8,128)(2,1)S(1)}, u32[]{:S(2)}, u32[]{:S(2)}) %collective-permute-start.2) | collective-permute-done | bytes 1179680 | tf_op jit(solution)/shard_map/ppermute | solution.py:696
  125.9 23.5 %collective-permute-done.1 = bf16[768,768]{0,1:T(8,128)(2,1)S(1)} collective-permute-done((bf16[768,768]{0,1:T(8,128)(2,1)S(1)}, bf16[768,768]{0,1:T(8,128)(2,1)S(1)}, u32[]{:S(2)}, u32[]{:S(2)}) %collective-permute-start.1) | collective-permute-done | bytes 1179680 | tf_op jit(solution)/shard_map/ppermute | solution.py:696
  149.5 3.6 convert_reduce_fusion.3
  153.0 2.0 convert_multiply_fusion
  155.1 24.0 %query_back.1 = bf16[768,384]{1,0:T(8,128)(2,1)} custom-call(s32[2,3]{1,0:T(2,128)} %pad_add_fusion.b_ref, bf16[3840,384]{1,0:T(8,128)(2,1)} %get-tuple-element.33.q_ref, bf16[3840,384]{1,0:T(8,128)(2,1)} %get-tuple-element.34.k_ref, bf16[3840,384]{1,0:T(8,128)(2,1)} %get-tuple-element.35.v_ref, bf16[768,384]{1,0:T(8,128)(2,1)} %get-tuple-element.36.o_ref, ...), custom_call_target="tpu_custom_call" | custom-call | tf_op jit(solution)/shard_map/query_back/pallas_call | solution.py:492
  180.4 3.4 fusion.33
  185.9 2.9 convolution_convert_fusion.7
  190.3 83.1 %back_halo.1 = (bf16[5,768,384]{2,1,0:T(8,128)(2,1)}, f32[5,16,768]{2,1,0:T(8,128)}) custom-call(bf16[768,384]{1,0:T(8,128)(2,1)} %get-tuple-element.140.g_ref.x_ref, f32[16,768]{1,0:T(8,128)} %concatenate.12.st_ref), custom_call_target="tpu_custom_call" | custom-call | tf_op jit(solution)/shard_map/back_halo/pallas_call | solution.py:333
  275.1 24.1 %key_back.1 = (bf16[768,384]{1,0:T(8,128)(2,1)}, bf16[768,384]{1,0:T(8,128)(2,1)}) custom-call(s32[2,3]{1,0:T(2,128)} %pad_add_fusion.b_ref, bf16[3840,384]{1,0:T(8,128)(2,1)} %get-tuple-element.33.q_ref, bf16[3840,384]{1,0:T(8,128)(2,1)} %get-tuple-element.34.k_ref, bf16[3840,384]{1,0:T(8,128)(2,1)} %get-tuple-element.35.v_ref, bf16[3840,384]{1,0:T(8,128)(2,1)} %bitcast.82, ...), custom_call_target="tpu_custom_call" | custom-call | tf_op jit(solution)/shard_map/key_back/pallas_call | solution.py:553
  309.3 21.3 %collective-permute-done.3 = bf16[768,768]{0,1:T(8,128)(2,1)S(1)} collective-permute-done((bf16[768,768]{0,1:T(8,128)(2,1)S(1)}, bf16[768,768]{0,1:T(8,128)(2,1)S(1)}, u32[]{:S(2)}, u32[]{:S(2)}) %collective-permute-start.3) | collective-permute-done | bytes 1179680 | tf_op jit(solution)/shard_map/ppermute | solution.py:696
  332.6 110.5 %ring_sum.1 = (bf16[768,1536]{1,0:T(8,128)(2,1)}, bf16[768,1536]{1,0:T(8,128)(2,1)}, bf16[1536,768]{1,0:T(8,128)(2,1)}, f32[128,128]{1,0:T(8,128)}) custom-call(bf16[768,1536]{1,0:T(8,128)(2,1)} %pad_maximum_fusion.refs_0_, bf16[768,1536]{1,0:T(8,128)(2,1)} %convolution_convert_fusion.1.refs_1_, bf16[1536,768]{1,0:T(8,128)(2,1)} %convolution_convert_fusion.refs_2_, ...), custom_call_target="tpu_custom_call" | custom-call | tf_op jit(solution)/shard_map/ring_sum/pallas_call | solution.py:678
  447.2 3.6 fusion.14
  452.8 3.5 convert_bitcast_fusion
  458.3 2.8 convert_element_type.170
  461.2 2.5 convert_element_type.171
  (168 shorter events, 53.0 us)
Async XLA Ops:
  71.1 3.4 copy-start.43
  71.1 4.0 copy-start.44
  71.1 4.6 copy-start.39
  71.1 13.0 %collective-permute-start = (bf16[768,384]{1,0:T(8,128)(2,1)}, bf16[768,384]{1,0:T(8,128)(2,1)}, u32[]{:S(2)}, u32[]{:S(2)}) collective-permute-start(bf16[768,384]{1,0:T(8,128)(2,1)} %get-tuple-element.36.o_ref), channel_id=1, source_target_pairs={{0,1},{1,0},{2,3},{3,2},{4,5},{5,4},{6,7},{7,6},{8,9},{9,8},{10,11... | collective-permute-start | bytes 1769480 | tf_op jit(solution)/shard_map/ppermute | solution.py:696
  73.2 10.9 %copy-start = (bf16[768,768]{0,1:T(8,128)(2,1)}, bf16[768,768]{0,1:T(8,128)(2,1)S(1)}, u32[]{:S(2)}) copy-start(bf16[768,768]{0,1:T(8,128)(2,1)S(1)} %copy.69) | copy-start | bytes 3538948
  73.2 6.2 %copy-start.5 = (bf16[768,384]{1,0:T(8,128)(2,1)S(1)}, bf16[768,384]{1,0:T(8,128)(2,1)}, u32[]{:S(2)}) copy-start(bf16[768,384]{1,0:T(8,128)(2,1)} %get-tuple-element.36.o_ref) | copy-start | bytes 1769476
  73.2 6.2 %copy-start.9 = (bf16[384,768]{1,0:T(8,128)(2,1)S(1)}, bf16[384,768]{1,0:T(8,128)(2,1)}, u32[]{:S(2)}) copy-start(bf16[384,768]{1,0:T(8,128)(2,1)} %wo_ref.1) | copy-start | bytes 1769476
  77.9 6.2 %copy-start.22 = (bf16[768,768]{1,0:T(8,128)(2,1)S(1)}, bf16[768,768]{1,0:T(8,128)(2,1)}, u32[]{:S(2)}) copy-start(bf16[768,768]{1,0:T(8,128)(2,1)} %get-tuple-element.37) | copy-start | bytes 3538948
  77.9 6.2 %copy-start.27 = (f32[768]{0:T(1024)S(1)}, f32[768]{0:T(1024)}, u32[]{:S(2)}) copy-start(f32[768]{0:T(1024)} %convert_element_type.133) | copy-start | bytes 9220
  97.8 26.4 %collective-permute-start.2 = (bf16[768,768]{0,1:T(8,128)(2,1)S(1)}, bf16[768,768]{0,1:T(8,128)(2,1)S(1)}, u32[]{:S(2)}, u32[]{:S(2)}) collective-permute-start(bf16[768,768]{0,1:T(8,128)(2,1)S(1)} %convolution_convert_fusion.2), channel_id=1, source_target_pairs={{0,1},{1,0},{2,3},{3,2},{4,5},{5,4},{6,7},{7,6},{8,9},{9,8},{10,11... | collective-permute-start | bytes 3538952 | tf_op jit(solution)/shard_map/ppermute | solution.py:696
  100.4 49.0 %collective-permute-start.1 = (bf16[768,768]{0,1:T(8,128)(2,1)S(1)}, bf16[768,768]{0,1:T(8,128)(2,1)S(1)}, u32[]{:S(2)}, u32[]{:S(2)}) collective-permute-start(bf16[768,768]{0,1:T(8,128)(2,1)S(1)} %convolution_convert_fusion.3), channel_id=1, source_target_pairs={{0,1},{1,0},{2,3},{3,2},{4,5},{5,4},{6,7},{7,6},{8,9},{9,8},{10,11... | collective-permute-start | bytes 3538952 | tf_op jit(solution)/shard_map/ppermute | solution.py:696
  109.2 40.3 %copy-start.26 = (f32[768]{0:T(1024)S(1)}, f32[768]{0:T(1024)}, u32[]{:S(2)}) copy-start(f32[768]{0:T(1024)} %convert_element_type.142) | copy-start | bytes 9220
  155.1 25.4 %copy-start.17 = (bf16[768,384]{1,0:T(8,128)(2,1)S(1)}, bf16[768,384]{1,0:T(8,128)(2,1)}, u32[]{:S(2)}) copy-start(bf16[768,384]{1,0:T(8,128)(2,1)} %wq_ref.1) | copy-start | bytes 1769476
  179.1 4.7 %copy-start.10 = (bf16[768,768]{0,1:T(8,128)(2,1)S(1)}, bf16[768,768]{0,1:T(8,128)(2,1)}, u32[]{:S(2)}) copy-start(bf16[768,768]{0,1:T(8,128)(2,1)} %get-tuple-element.116) | copy-start | bytes 3538948
  180.4 5.1 %copy-start.12 = (f32[768,384]{1,0:T(8,128)S(1)}, f32[768,384]{1,0:T(8,128)}, u32[]{:S(2)}) copy-start(f32[768,384]{1,0:T(8,128)} %get-tuple-element.139) | copy-start | bytes 3538948
  275.1 25.5 %copy-start.18 = (bf16[768,384]{1,0:T(8,128)(2,1)S(1)}, bf16[768,384]{1,0:T(8,128)(2,1)}, u32[]{:S(2)}) copy-start(bf16[768,384]{1,0:T(8,128)(2,1)} %wk_ref.1) | copy-start | bytes 1769476
  299.2 3.3 copy-start.16
  303.4 27.2 %copy-start.4 = (bf16[768,768]{0,1:T(8,128)(2,1)}, bf16[768,768]{0,1:T(8,128)(2,1)S(1)}, u32[]{:S(2)}) copy-start(bf16[768,768]{0,1:T(8,128)(2,1)S(1)} %add_convert_fusion) | copy-start | bytes 3538948
  303.4 27.2 %collective-permute-start.3 = (bf16[768,768]{0,1:T(8,128)(2,1)S(1)}, bf16[768,768]{0,1:T(8,128)(2,1)S(1)}, u32[]{:S(2)}, u32[]{:S(2)}) collective-permute-start(bf16[768,768]{0,1:T(8,128)(2,1)S(1)} %add_convert_fusion), channel_id=1, source_target_pairs={{0,1},{1,0},{2,3},{3,2},{4,5},{5,4},{6,7},{7,6},{8,9},{9,8},{10,11... | collective-permute-start | bytes 3538952 | tf_op jit(solution)/shard_map/ppermute | solution.py:696
  307.7 22.9 %copy-start.1 = (bf16[768,768]{0,1:T(8,128)(2,1)S(1)}, bf16[768,768]{0,1:T(8,128)(2,1)}, u32[]{:S(2)}) copy-start(bf16[768,768]{0,1:T(8,128)(2,1)} %copy-done) | copy-start | bytes 3538948
  309.3 22.6 %copy-start.38 = (f32[1536]{0:T(1024)S(1)}, f32[1536]{0:T(1024)}, u32[]{:S(2)}) copy-start(f32[1536]{0:T(1024)} %get-tuple-element.141) | copy-start | bytes 18436
  309.3 22.6 %copy-start.24 = (f32[768]{0:T(1024)S(1)}, f32[768]{0:T(1024)}, u32[]{:S(2)}) copy-start(f32[768]{0:T(1024)} %get-tuple-element.117) | copy-start | bytes 9220
  309.3 22.6 %copy-start.29 = (f32[768]{0:T(1024)S(1)}, f32[768]{0:T(1024)}, u32[]{:S(2)}) copy-start(f32[768]{0:T(1024)} %get-tuple-element.100) | copy-start | bytes 9220
  309.3 22.6 %copy-start.28 = (f32[768]{0:T(1024)S(1)}, f32[768]{0:T(1024)}, u32[]{:S(2)}) copy-start(f32[768]{0:T(1024)} %get-tuple-element.106) | copy-start | bytes 9220
  (28 other events, 63.1 us)

commit v2 on v1

--- a/solution.py
+++ b/solution.py
@@ -10,13 +10,19 @@
 HEAD_DIM = 64
 REACH = 2
 TILE = 256
-PIECES = 3
-NEG = -1e30
+PIECES = 6
+AHEAD = 2
+NEG = -3e38
+CLIPS = 64
+LOGS = 64
+CENTRES = 96
+FAR = -(2.0**100)
+SAFE = 40.0
 BF = jnp.bfloat16
 F32 = jnp.float32
 MESH = pl.DeviceIdType.MESH
 VMEM = pltpu.VMEM
-VMEM_BYTES = 66_000_000
+VMEM_BYTES = 26_000_000
 DMA = pltpu.SemaphoreType.DMA
 
 
@@ -82,7 +88,7 @@
 
 def halo_kernel(
     x_ref, wo_ref, gain_ref, shift_ref, wq_ref, wk_ref, wv_ref, qb_ref, vb_ref,
-    q_ref, k_ref, v_ref, a_ref, wof_ref,
+    q_ref, k_ref, v_ref, a_ref, wof_ref, n_ref,
     win, sx, rx, sy, ry, ss, rs, sf, rf, sw, rw, sv, rv,
 ):
     d, core, has_left, has_right = place()
@@ -126,24 +132,39 @@
     w_copy = remote(wo_ref.at[wo_rows], wof_ref.at[full_rows(t)], sw, rw, across)
     wf_copy = remote(wof_ref.at[full_rows(1 - t)], wof_ref.at[full_rows(1 - t)], sv, rv, sibling)
 
-    for p in range(PIECES):
+    def send(p):
         for side in (0, 1):
 
             @pl.when(exists[1 - side])
             def _():
                 x_copy(side, p).start()
 
+    for p in range(AHEAD):
+        send(p)
+    w_copy.start()
     own_copy.start()
     gain, shift = gain_ref[...].astype(F32), shift_ref[...].astype(F32)
     query_bias, value_bias = qb_ref[...].astype(F32), vb_ref[...].astype(F32)
+
+    n_ref[...] = jnp.zeros(n_ref.shape, F32)
+
+    def raise_norm(spot, values):
+        for c in range(values.shape[1] // 128):
+            part = values[:, c * 128 : c * 128 + 128]
+            norm = jnp.max(jnp.sum(part * part, axis=1, keepdims=True), axis=0, keepdims=True)
+            n_ref[spot, :] = jnp.maximum(n_ref[spot, :], norm)
 
     def project(values, slot, start, keep=False):
         attn = (norm_rows(values.astype(F32)) * gain + shift).astype(BF)
         out = pl.ds(pl.multiple_of(slot * height + start, 128), half)
         if keep:
             a_ref[pl.ds(pl.multiple_of(start, half), half), :] = attn
-        q_ref[out, :] = ((dot_nn(attn, wq_ref[...]) + query_bias) * HEAD_DIM**-0.5).astype(BF)
-        k_ref[out, :] = dot_nn(attn, wk_ref[...]).astype(BF)
+        query = (dot_nn(attn, wq_ref[...]) + query_bias) * HEAD_DIM**-0.5
+        key = dot_nn(attn, wk_ref[...])
+        q_ref[out, :] = query.astype(BF)
+        k_ref[out, :] = key.astype(BF)
+        raise_norm(slice(0, 8), query)
+        raise_norm(slice(8, 16), key)
         v_ref[out, :] = (dot_nn(attn, wv_ref[...]) + value_bias).astype(BF)
 
     def project_half(slot, which):
@@ -173,14 +194,20 @@
             def _():
                 f_copy(0, p).start()
 
+        if p + AHEAD < PIECES:
+            send(p + AHEAD)
+
     lax.fori_loop(0, 2, own_step, 0)
     wof_ref[pl.ds(pl.multiple_of(t * 2 * part, part), 2 * part), :] = wo_ref[...]
     pass_on(0)
+    w_copy.wait_recv()
+    wf_copy.start()
+    for p in range(1, PIECES // 2):
+        pass_on(p)
     own_copy.wait_recv()
     project_block(3 - 2 * core)
-    for p in range(1, PIECES):
+    for p in range(PIECES // 2, PIECES):
         pass_on(p)
-    w_copy.start()
     for side in (0, 1):
 
         @pl.when(exists[side])
@@ -198,8 +225,6 @@
             def _():
                 f_copy(1, p).start()
 
-    w_copy.wait_recv()
-    wf_copy.start()
     for side in (0, 1):
 
         @pl.when(exists[side])
@@ -245,9 +270,10 @@
             wide, wide, wide,
             jax.ShapeDtypeStruct((height, width), BF),
             jax.ShapeDtypeStruct((2 * wo.shape[0], wo.shape[1]), BF),
+            jax.ShapeDtypeStruct((16, 128), F32),
         ),
         in_specs=[whole()] * 9,
-        out_specs=[whole()] * 5,
+        out_specs=[whole()] * 6,
         scratch_shapes=[pltpu.VMEM((blocks, height, width), BF)]
         + [pair, pair, pair, pair, DMA, DMA, pair, pair, DMA, DMA, DMA, DMA],
         compiler_params=pltpu.CompilerParams(
@@ -257,9 +283,30 @@
     )(x, wo, gain, shift, wq, wk, wv, qb, vb)
 
 
-def back_halo_kernel(x_ref, st_ref, xw_ref, sw_ref, sx, rx, ss, rs, sf, rf):
+def split3(values):
+    first = values.astype(BF).astype(F32)
+    second = (values - first).astype(BF).astype(F32)
+    return first, second, values - first - second
+
+
+def code_tile(rows, keys_code):
+    count = rows.shape[1]
+    terms = split3(-rows)
+    lane = lax.broadcasted_iota(jnp.int32, (128, count), 0)
+    tall = jnp.zeros((128, count), F32)
+    for h in range(8):
+        for base, row in ((LOGS, h), (CENTRES, 8 + h)):
+            for i in range(3):
+                tall = jnp.where(lane == base + 3 * h + i, terms[i][row : row + 1], tall)
+    wide = jnp.transpose(tall)
+    column = lax.broadcasted_iota(jnp.int32, wide.shape, 1)
+    same = jnp.logical_and(column < CLIPS, keys_code.astype(F32) == 0.0)
+    return jnp.where(same, 1.0, wide).astype(BF)
+
+
+def back_halo_kernel(x_ref, o_ref, lse_ref, kc_ref, xw_ref, qc_ref, st_ref, sw_ref, sx, rx, ss, rs, sf, rf):
     d, core, has_left, has_right = place()
-    height = x_ref.shape[0]
+    height, cols = x_ref.shape
     piece = height // PIECES
     sibling = {"dp": d + 1 - 2 * core}
     exists = (has_left, has_right)
@@ -287,18 +334,41 @@
         _, dst = refs(p)
         return remote(dst(4 - 4 * core), dst(3 - 2 * core), sf.at[p], rf.at[p], sibling)
 
-    order = (PIECES,) + tuple(range(PIECES))
-    for p in order:
+    order = tuple(range(PIECES)) + (PIECES,)
+
+    def send(p):
         for side in (0, 1):
 
             @pl.when(exists[1 - side])
             def _():
                 x_copy(side, p).start()
 
-    for p in order:
         s_copy(p).start()
+
+    for p in range(PIECES):
+        send(p)
+    picks = lax.broadcasted_iota(jnp.int32, (8, cols), 1) // HEAD_DIM
+    picks = (picks == lax.broadcasted_iota(jnp.int32, (8, cols), 0)).astype(F32)
+    product = x_ref[...].astype(F32) * o_ref[...].astype(F32)
+    st_ref[0:8, :] = lse_ref[...]
+    st_ref[8:16, :] = lax.dot_general(
+        picks, product, (((1,), (1,)), ((), ())),
+        precision=lax.Precision.HIGHEST, preferred_element_type=F32,
+    )
+    send(PIECES)
     xw_ref[REACH] = x_ref[...]
     sw_ref[REACH] = st_ref[...]
+
+    def code(slot):
+        def step(i, carry):
+            rows = pl.ds(pl.multiple_of(slot * height + i * TILE, TILE), TILE)
+            stats = sw_ref[slot, :, pl.ds(pl.multiple_of(i * TILE, TILE), TILE)]
+            qc_ref[rows, :] = code_tile(stats, kc_ref[rows, :])
+            return carry
+
+        lax.fori_loop(0, height // TILE, step, 0)
+
+    code(REACH)
     for p in order:
         for side in (0, 1):
 
@@ -326,237 +396,257 @@
             def _():
                 f_copy(p).wait_recv()
 
-
-def back_halo(x, stats):
+    code(3 - 2 * core)
+    for side in (0, 1):
+
+        @pl.when(exists[side])
+        def _():
+            code(slots[side])
+
+        @pl.when(jnp.logical_and(exists[side], core == side))
+        def _():
+            code(1 + 2 * core)
+
+
+def back_halo(x, o, lse, kc):
     blocks = 2 * REACH + 1
+    height = x.shape[0]
     pair, line = DMA((2, PIECES + 1)), DMA((PIECES + 1,))
     return pl.pallas_call(
         back_halo_kernel,
         out_shape=(
             jax.ShapeDtypeStruct((blocks,) + x.shape, x.dtype),
-            jax.ShapeDtypeStruct((blocks,) + stats.shape, stats.dtype),
+            jax.ShapeDtypeStruct(kc.shape, BF),
         ),
-        in_specs=[whole()] * 2,
+        in_specs=[whole()] * 4,
         out_specs=[whole()] * 2,
-        scratch_shapes=[pair, pair, line, line, line, line],
+        scratch_shapes=[
+            pltpu.VMEM((16, height), F32), pltpu.VMEM((blocks, 16, height), F32),
+            pair, pair, line, line, line, line,
+        ],
         compiler_params=pltpu.CompilerParams(
             collective_id=1, has_side_effects=True, vmem_limit_bytes=VMEM_BYTES
         ),
         name="back_halo",
-    )(x, stats)
-
-
-def only(values, lower, keep_low):
-    return jnp.where(lower if keep_low else jnp.logical_not(lower), values, jnp.zeros_like(values))
-
-
-def low_lanes(shape):
-    return lax.broadcasted_iota(jnp.int32, shape, 1) < HEAD_DIM
-
-
-def key_tile(j):
+    )(x, o, lse, kc)
+
+
+def tile_at(j):
     return pl.ds(pl.multiple_of(j * TILE, TILE), TILE)
 
 
-def attend_kernel(b_ref, q_ref, k_ref, v_ref, own_ref, win_ref, o_ref, lse_ref, row_ref, s_ref, m_ref, l_ref, acc_ref):
-    i = pl.program_id(1)
-    lo, hi = b_ref[0, i], b_ref[1, i]
-    lower = low_lanes((TILE, 128))
-    query = q_ref[...]
-    queries = (only(query, lower, True), only(query, lower, False))
-    own = own_ref[...]
-    m_ref[...] = jnp.full(m_ref.shape, NEG, F32)
-    l_ref[...] = jnp.zeros(l_ref.shape, F32)
-    acc_ref[...] = jnp.zeros(acc_ref.shape, F32)
-
-    def score(j, carry):
-        keys = k_ref[key_tile(j), :]
-        same = own == win_ref[j]
-        for h in (0, 1):
-            s = jnp.where(same, dot_nt(queries[h], keys), NEG)
-            s_ref[h, j - lo] = s
-            m_ref[h] = jnp.maximum(m_ref[h], jnp.maximum(s[:, :128], s[:, 128:]))
+def lanes_of(c):
+    return pl.ds(c * 128, 128)
+
+
+def beside(left, right):
+    return jnp.concatenate([left, right], axis=1)
+
+
+def stacked_heads(values, codes):
+    lower = lax.broadcasted_iota(jnp.int32, values.shape, 1) < HEAD_DIM
+    none = jnp.zeros_like(values)
+    return jnp.concatenate(
+        [beside(jnp.where(lower, values, none), codes[0]), beside(jnp.where(lower, none, values), codes[1])],
+        axis=0,
+    )
+
+
+def heads_out(turned):
+    pair = jnp.concatenate([turned[:HEAD_DIM, :TILE], turned[HEAD_DIM:, TILE:]], axis=0)
+    return jnp.transpose(pair)
+
+
+def within(lane, start):
+    return jnp.logical_and(lane >= start, lane < start + 3)
+
+
+def attend_kernel(b_ref, q_ref, k_ref, v_ref, kc_ref, n_ref, o_ref, lse_ref, r_ref, m_ref, l_ref, acc_ref):
+    height, cols = o_ref.shape
+    pairs, tiles = cols // 128, height // TILE
+    steep = jnp.logical_not(jnp.max(n_ref[0:8, :]) * jnp.max(n_ref[8:16, :]) <= SAFE * SAFE)
+    lane = lax.broadcasted_iota(jnp.int32, (TILE, 128), 1)
+
+    def groups(values):
+        return values.reshape(TILE // 8, 8, values.shape[1])
+
+    def one(i, carry):
+        lo, hi = b_ref[0, i], b_ref[1, i]
+        own = pl.ds(pl.multiple_of(REACH * height + i * TILE, TILE), TILE)
+        same = jnp.logical_and(lane < CLIPS, kc_ref[own, :].astype(F32) == 0.0)
+        code = jnp.where(same, 1.0, 0.0).astype(BF)
+        for c in range(pairs):
+            r_ref[c] = stacked_heads(q_ref[own, lanes_of(c)], (code, code))
+        acc_ref[...] = jnp.zeros(acc_ref.shape, F32)
+        l_ref[...] = jnp.zeros(l_ref.shape, F32)
+        m_ref[...] = jnp.zeros(m_ref.shape, F32)
+
+        def score(j, c):
+            return dot_nt(beside(k_ref[tile_at(j), lanes_of(c)], kc_ref[tile_at(j), :]), r_ref[c])
+
+        def step(shift, j, carry):
+            raised = []
+            for c in range(pairs):
+                s = score(j, c)
+                e = jnp.exp(s - m_ref[c, 0:1, :] if shift else s)
+                l_ref[c] += jnp.sum(groups(e), axis=0)
+                raised.append(e.astype(BF))
+            for c in range(pairs):
+                acc_ref[c] += dot_tn(v_ref[tile_at(j), lanes_of(c)], raised[c])
+            return carry
+
+        @pl.when(jnp.logical_not(steep))
+        def _():
+            lax.fori_loop(lo, hi, functools.partial(step, False), 0)
+
+        @pl.when(steep)
+        def _():
+            m_ref[...] = jnp.full(m_ref.shape, NEG, F32)
+
+            def peak(j, carry):
+                for c in range(pairs):
+                    m_ref[c] = jnp.maximum(m_ref[c], jnp.max(groups(score(j, c)), axis=0))
+                return carry
+
+            lax.fori_loop(lo, hi, peak, 0)
+            for c in range(pairs):
+                m_ref[c] = jnp.broadcast_to(jnp.max(m_ref[c], axis=0, keepdims=True), m_ref.shape[1:])
+            lax.fori_loop(lo, hi, functools.partial(step, True), 0)
+
+        for c in range(pairs):
+            total = jnp.sum(l_ref[c], axis=0, keepdims=True)
+            o_ref[tile_at(i), lanes_of(c)] = heads_out(acc_ref[c] / total).astype(BF)
+            logs = m_ref[c, 0:1, :] + jnp.log(total)
+            lse_ref[2 * c : 2 * c + 1, tile_at(i)] = logs[:, :TILE]
+            lse_ref[2 * c + 1 : 2 * c + 2, tile_at(i)] = logs[:, TILE:]
         return carry
 
-    lax.fori_loop(lo, hi, score, 0)
-    tops = [jnp.max(m_ref[h], axis=1, keepdims=True) for h in (0, 1)]
-
-    def weigh(j, carry):
-        values = v_ref[key_tile(j), :]
-        for h in (0, 1):
-            e = jnp.exp(s_ref[h, j - lo] - tops[h])
-            l_ref[h] += e[:, :128] + e[:, 128:]
-            acc_ref[h] += dot_nn(e.astype(BF), values)
-        return carry
-
-    lax.fori_loop(lo, hi, weigh, 0)
-    totals = [jnp.sum(l_ref[h], axis=1, keepdims=True) for h in (0, 1)]
-    o_ref[...] = jnp.where(lower, acc_ref[0] / totals[0], acc_ref[1] / totals[1]).astype(BF)
-    logs = jnp.where(lower, tops[0] + jnp.log(totals[0]), tops[1] + jnp.log(totals[1]))
-    lse_ref[0] = logs
-    turned = jnp.transpose(logs)
-    row_ref[0, 0:8, :] = turned[0:8]
-    row_ref[0, 8:16, :] = turned[HEAD_DIM : HEAD_DIM + 8]
-
-
-def attend(bounds, q, k, v, own, win):
-    window, cols = k.shape
-    tiles = own.shape[0] // TILE
-    pairs = cols // 128
-    first = REACH * tiles
-    most = 2 * REACH * tiles + tiles
+    lse_ref[...] = jnp.zeros(lse_ref.shape, F32)
+    lax.fori_loop(0, tiles, one, 0)
+
+
+def local_call(kernel, name, out_shape, scratch, bounds, *values):
     grid = pltpu.PrefetchScalarGridSpec(
         num_scalar_prefetch=1,
-        grid=(pairs, tiles),
-        in_specs=[
-            pl.BlockSpec((TILE, 128), lambda p, i, b: (first + i, p)),
-            pl.BlockSpec((window, 128), lambda p, i, b: (0, p)),
-            pl.BlockSpec((window, 128), lambda p, i, b: (0, p)),
-            pl.BlockSpec((TILE, 1), lambda p, i, b: (i, 0)),
-            pl.BlockSpec(win.shape, lambda p, i, b: (0, 0, 0)),
-        ],
-        out_specs=[
-            pl.BlockSpec((TILE, 128), lambda p, i, b: (i, p)),
-            pl.BlockSpec((1, TILE, 128), lambda p, i, b: (p, i, 0)),
-            pl.BlockSpec((1, 16, TILE), lambda p, i, b: (p, 0, i)),
-        ],
-        scratch_shapes=[
-            pltpu.VMEM((2, most, TILE, TILE), F32),
-            pltpu.VMEM((2, TILE, 128), F32),
-            pltpu.VMEM((2, TILE, 128), F32),
-            pltpu.VMEM((2, TILE, 128), F32),
-        ],
+        grid=(1,),
+        in_specs=[whole()] * len(values),
+        out_specs=jax.tree.map(lambda _: whole(), out_shape),
+        scratch_shapes=scratch,
     )
     return pl.pallas_call(
-        attend_kernel,
+        kernel,
         grid_spec=grid,
-        out_shape=(
-            jax.ShapeDtypeStruct((tiles * TILE, cols), BF),
-            jax.ShapeDtypeStruct((pairs, tiles * TILE, 128), F32),
-            jax.ShapeDtypeStruct((pairs, 16, tiles * TILE), F32),
-        ),
+        out_shape=out_shape,
         compiler_params=pltpu.CompilerParams(vmem_limit_bytes=VMEM_BYTES),
-        name="attend",
-    )(bounds, q, k, v, own, win)
-
-
-def query_back_kernel(b_ref, q_ref, k_ref, v_ref, o_ref, g_ref, lse_ref, own_ref, win_ref, dq_ref, acc_ref):
-    i = pl.program_id(1)
-    lo, hi = b_ref[0, i], b_ref[1, i]
-    lower = low_lanes((TILE, 128))
-    query, grad = q_ref[...], g_ref[...]
-    queries = (only(query, lower, True), only(query, lower, False))
-    grads = (only(grad, lower, True), only(grad, lower, False))
-    product = grad.astype(F32) * o_ref[...].astype(F32)
-    centres = [jnp.sum(only(product, lower, h == 0), axis=1, keepdims=True) for h in (0, 1)]
-    logs = [lse_ref[0, :, 0:1], lse_ref[0, :, HEAD_DIM : HEAD_DIM + 1]]
-    own = own_ref[...]
-    acc_ref[...] = jnp.zeros(acc_ref.shape, F32)
-
-    def step(j, carry):
-        keys, values = k_ref[key_tile(j), :], v_ref[key_tile(j), :]
-        same = own == win_ref[j]
-        for h in (0, 1):
-            s = jnp.where(same, dot_nt(queries[h], keys), NEG)
-            probs = jnp.exp(s - logs[h])
-            d_score = probs * (dot_nt(grads[h], values) - centres[h])
-            acc_ref[h] += dot_nn(d_score.astype(BF), keys)
+        name=name,
+    )(bounds, *values)
+
+
+def attend(bounds, q, k, v, kc, norms, height):
+    cols = k.shape[1]
+    pairs = cols // 128
+    out_shape = (jax.ShapeDtypeStruct((height, cols), BF), jax.ShapeDtypeStruct((8, height), F32))
+    scratch = [
+        pltpu.VMEM((pairs, 2 * TILE, 256), BF),
+        pltpu.VMEM((pairs, 8, 2 * TILE), F32),
+        pltpu.VMEM((pairs, 8, 2 * TILE), F32),
+        pltpu.VMEM((pairs, 128, 2 * TILE), F32),
+    ]
+    return local_call(attend_kernel, "attend", out_shape, scratch, bounds, q, k, v, kc, norms)
+
+
+def query_back_kernel(b_ref, q_ref, k_ref, v_ref, g_ref, kc_ref, qc_ref, dq_ref, r_ref, t_ref, acc_ref):
+    height, cols = dq_ref.shape
+    pairs, tiles = cols // 128, height // TILE
+    lane = lax.broadcasted_iota(jnp.int32, (TILE, 128), 1)
+
+    def one(i, carry):
+        own = pl.ds(pl.multiple_of(REACH * height + i * TILE, TILE), TILE)
+        code = qc_ref[own, :]
+        none = jnp.zeros_like(code)
+        for c in range(pairs):
+            logs, centres = [], []
+            for h in (2 * c, 2 * c + 1):
+                logs.append(jnp.where(jnp.logical_or(lane < CLIPS, within(lane, LOGS + 3 * h)), code, none))
+                centres.append(jnp.where(within(lane, CENTRES + 3 * h), code, none))
+            r_ref[c] = stacked_heads(q_ref[own, lanes_of(c)], logs)
+            t_ref[c] = stacked_heads(g_ref[own, lanes_of(c)], centres)
+        acc_ref[...] = jnp.zeros(acc_ref.shape, F32)
+
+        def step(j, carry):
+            code = kc_ref[tile_at(j), :]
+            steps = []
+            for c in range(pairs):
+                probs = jnp.exp(dot_nt(beside(k_ref[tile_at(j), lanes_of(c)], code), r_ref[c]))
+                d_probs = dot_nt(beside(v_ref[tile_at(j), lanes_of(c)], code), t_ref[c])
+                steps.append((probs * d_probs).astype(BF))
+            for c in range(pairs):
+                acc_ref[c] += dot_tn(k_ref[tile_at(j), lanes_of(c)], steps[c])
+            return carry
+
+        lax.fori_loop(b_ref[0, i], b_ref[1, i], step, 0)
+        for c in range(pairs):
+            dq_ref[tile_at(i), lanes_of(c)] = (heads_out(acc_ref[c]) * HEAD_DIM**-0.5).astype(BF)
         return carry
 
-    lax.fori_loop(lo, hi, step, 0)
-    dq_ref[...] = (jnp.where(lower, acc_ref[0], acc_ref[1]) * HEAD_DIM**-0.5).astype(BF)
-
-
-def query_back(bounds, q, k, v, o, g, lse, own, win):
-    window, cols = k.shape
-    tiles = own.shape[0] // TILE
+    lax.fori_loop(0, tiles, one, 0)
+
+
+def query_back(bounds, q, k, v, g, kc, qc, height):
+    cols = k.shape[1]
     pairs = cols // 128
-    first = REACH * tiles
-    tile = pl.BlockSpec((TILE, 128), lambda p, i, b: (i, p))
-    grid = pltpu.PrefetchScalarGridSpec(
-        num_scalar_prefetch=1,
-        grid=(pairs, tiles),
-        in_specs=[
-            pl.BlockSpec((TILE, 128), lambda p, i, b: (first + i, p)),
-            pl.BlockSpec((window, 128), lambda p, i, b: (0, p)),
-            pl.BlockSpec((window, 128), lambda p, i, b: (0, p)),
-            tile,
-            tile,
-            pl.BlockSpec((1, TILE, 128), lambda p, i, b: (p, i, 0)),
-            pl.BlockSpec((TILE, 1), lambda p, i, b: (i, 0)),
-            pl.BlockSpec(win.shape, lambda p, i, b: (0, 0, 0)),
-        ],
-        out_specs=tile,
-        scratch_shapes=[pltpu.VMEM((2, TILE, 128), F32)],
-    )
-    return pl.pallas_call(
-        query_back_kernel,
-        grid_spec=grid,
-        out_shape=jax.ShapeDtypeStruct((tiles * TILE, cols), BF),
-        compiler_params=pltpu.CompilerParams(vmem_limit_bytes=VMEM_BYTES),
-        name="query_back",
-    )(bounds, q, k, v, o, g, lse, own, win)
-
-
-def key_back_kernel(b_ref, q_ref, k_ref, v_ref, g_ref, st_ref, own_ref, win_ref, dk_ref, dv_ref, acck_ref, accv_ref):
-    p, i = pl.program_id(0), pl.program_id(1)
-    lo, hi = b_ref[0, i], b_ref[1, i]
-    lower = low_lanes((TILE, 128))
-    key, value = k_ref[...], v_ref[...]
-    keys = (only(key, lower, True), only(key, lower, False))
-    values = (only(value, lower, True), only(value, lower, False))
-    own = own_ref[...]
-    acck_ref[...] = jnp.zeros(acck_ref.shape, F32)
-    accv_ref[...] = jnp.zeros(accv_ref.shape, F32)
-
-    def step(j, carry):
-        queries, grads = q_ref[key_tile(j), :], g_ref[key_tile(j), :]
-        same = own == win_ref[j]
-        for h in (0, 1):
-            logs = st_ref[j, pl.ds(2 * p + h, 1), :]
-            centres = st_ref[j, pl.ds(8 + 2 * p + h, 1), :]
-            s = jnp.where(same, dot_nt(keys[h], queries), NEG)
-            probs = jnp.exp(s - logs)
-            d_score = probs * (dot_nt(values[h], grads) - centres)
-            accv_ref[h] += dot_nn(probs.astype(BF), grads)
-            acck_ref[h] += dot_nn(d_score.astype(BF), queries)
+    scratch = [pltpu.VMEM((pairs, 2 * TILE, 256), BF)] * 2 + [pltpu.VMEM((pairs, 128, 2 * TILE), F32)]
+    out_shape = jax.ShapeDtypeStruct((height, cols), BF)
+    return local_call(query_back_kernel, "query_back", out_shape, scratch, bounds, q, k, v, g, kc, qc)
+
+
+def key_back_kernel(b_ref, q_ref, k_ref, v_ref, g_ref, kc_ref, qc_ref, dk_ref, dv_ref, r_ref, t_ref, ak_ref, av_ref):
+    height, cols = dk_ref.shape
+    pairs, tiles = cols // 128, height // TILE
+    lane = lax.broadcasted_iota(jnp.int32, (TILE, 128), 1)
+
+    def one(i, carry):
+        own = pl.ds(pl.multiple_of(REACH * height + i * TILE, TILE), TILE)
+        code = kc_ref[own, :]
+        none, ones = jnp.zeros_like(code), jnp.ones_like(code)
+        for c in range(pairs):
+            logs, centres = [], []
+            for h in (2 * c, 2 * c + 1):
+                logs.append(jnp.where(lane < CLIPS, code, jnp.where(within(lane, LOGS + 3 * h), ones, none)))
+                centres.append(jnp.where(within(lane, CENTRES + 3 * h), ones, none))
+            r_ref[c] = stacked_heads(k_ref[own, lanes_of(c)], logs)
+            t_ref[c] = stacked_heads(v_ref[own, lanes_of(c)], centres)
+        ak_ref[...] = jnp.zeros(ak_ref.shape, F32)
+        av_ref[...] = jnp.zeros(av_ref.shape, F32)
+
+        def step(j, carry):
+            code = qc_ref[tile_at(j), :]
+            weights, steps = [], []
+            for c in range(pairs):
+                probs = jnp.exp(dot_nt(beside(q_ref[tile_at(j), lanes_of(c)], code), r_ref[c]))
+                d_probs = dot_nt(beside(g_ref[tile_at(j), lanes_of(c)], code), t_ref[c])
+                weights.append(probs.astype(BF))
+                steps.append((probs * d_probs).astype(BF))
+            for c in range(pairs):
+                av_ref[c] += dot_tn(g_ref[tile_at(j), lanes_of(c)], weights[c])
+                ak_ref[c] += dot_tn(q_ref[tile_at(j), lanes_of(c)], steps[c])
+            return carry
+
+        lax.fori_loop(b_ref[0, i], b_ref[1, i], step, 0)
+        for c in range(pairs):
+            dk_ref[tile_at(i), lanes_of(c)] = heads_out(ak_ref[c]).astype(BF)
+            dv_ref[tile_at(i), lanes_of(c)] = heads_out(av_ref[c]).astype(BF)
         return carry
 
-    lax.fori_loop(lo, hi, step, 0)
-    dk_ref[...] = jnp.where(lower, acck_ref[0], acck_ref[1]).astype(BF)
-    dv_ref[...] = jnp.where(lower, accv_ref[0], accv_ref[1]).astype(BF)
-
-
-def key_back(bounds, q, k, v, g, stats, own, win):
-    window, cols = k.shape
-    tiles = own.shape[0] // TILE
+    lax.fori_loop(0, tiles, one, 0)
+
+
+def key_back(bounds, q, k, v, g, kc, qc, height):
+    cols = k.shape[1]
     pairs = cols // 128
-    first = REACH * tiles
-    tile = pl.BlockSpec((TILE, 128), lambda p, i, b: (i, p))
-    centre = pl.BlockSpec((TILE, 128), lambda p, i, b: (first + i, p))
-    strip = pl.BlockSpec((window, 128), lambda p, i, b: (0, p))
-    grid = pltpu.PrefetchScalarGridSpec(
-        num_scalar_prefetch=1,
-        grid=(pairs, tiles),
-        in_specs=[
-            strip,
-            centre,
-            centre,
-            strip,
-            pl.BlockSpec(stats.shape, lambda p, i, b: (0, 0, 0)),
-            pl.BlockSpec((TILE, 1), lambda p, i, b: (i, 0)),
-            pl.BlockSpec(win.shape, lambda p, i, b: (0, 0, 0)),
-        ],
-        out_specs=[tile, tile],
-        scratch_shapes=[pltpu.VMEM((2, TILE, 128), F32), pltpu.VMEM((2, TILE, 128), F32)],
-    )
-    return pl.pallas_call(
-        key_back_kernel,
-        grid_spec=grid,
-        out_shape=(jax.ShapeDtypeStruct((tiles * TILE, cols), BF),) * 2,
-        compiler_params=pltpu.CompilerParams(vmem_limit_bytes=VMEM_BYTES),
-        name="key_back",
-    )(bounds, q, k, v, g, stats, own, win)
+    scratch = [pltpu.VMEM((pairs, 2 * TILE, 256), BF)] * 2 + [pltpu.VMEM((pairs, 128, 2 * TILE), F32)] * 2
+    out_shape = (jax.ShapeDtypeStruct((height, cols), BF),) * 2
+    return local_call(key_back_kernel, "key_back", out_shape, scratch, bounds, q, k, v, g, kc, qc)
 
 
 def ring_kernel(arrays, *refs):
@@ -711,11 +801,9 @@
     w_out, out_bias, mlp_gain, mlp_shift, w_fc1, fc1_bias, w_fc2, fc2_bias, cotangent,
 ):
     height, width = inputs.shape
-    tiles = height // TILE
     d = lax.axis_index("dp")
     t = lax.axis_index("tensor")
     reach = REACH * height
-    heads = w_query.shape[1] // HEAD_DIM
 
     padded = jnp.pad(clip_ids, (reach, reach), constant_values=-1)
     window = lax.dynamic_slice_in_dim(padded, d * height, height + 2 * reach)
@@ -725,17 +813,17 @@
     begin = jnp.sum((clip_ids[None, :] < firsts[:, None]).astype(jnp.int32), axis=1) - origin
     end = jnp.sum((clip_ids[None, :] <= lasts[:, None]).astype(jnp.int32), axis=1) - origin
     bounds = jnp.stack([begin // TILE, (end + TILE - 1) // TILE])
-    own = own[:, None]
-    window = window.reshape(-1, 1, TILE)
+    lane = jnp.arange(128, dtype=jnp.int32)[None, :]
+    clip_far = jnp.where(window[:, None] == lane, 0.0, FAR)
+    key_code = jnp.where(lane < CLIPS, clip_far, 1.0).astype(BF)
 
     row = lambda v: v[None, :]
-    q, k, v, attn_input, w_out_full = halo_qkv(
+    q, k, v, attn_input, w_out_full, norms = halo_qkv(
         inputs, w_out, row(attn_gain), row(attn_shift), w_query, w_key, w_value,
         row(query_bias), row(value_bias),
     )
-    mixed, lse, lse_rows = attend(bounds, q, k, v, own, window)
+    mixed, logs = attend(bounds, q, k, v, key_code, norms, height)
     other = swapped(mixed)
-    flip = t == 0
     w_mine = w_out
     w_other = lax.dynamic_slice_in_dim(w_out_full, (1 - t) * w_out.shape[0], w_out.shape[0])
     source = inputs.astype(F32)
@@ -766,16 +854,10 @@
     fc1_bias_grad = jnp.sum(pre_grad.astype(F32), axis=0)
     out_bias_grad = jnp.sum(attn_grad_low.astype(F32), axis=0)
 
-    product = (mixed_grad.astype(F32) * mixed.astype(F32)).reshape(height, heads, HEAD_DIM)
-    centres = jnp.sum(product, axis=2).T
-    logs = jnp.stack([lse_rows[h // 2, 8 * (h % 2)] for h in range(heads)])
-    gap = jnp.zeros((8 - heads, height), F32)
-    stats = jnp.concatenate([logs, gap, centres, gap])
-    grad_win, stat_win = back_halo(mixed_grad, stats)
+    grad_win, query_code = back_halo(mixed_grad, mixed, logs, key_code)
     grad_win = grad_win.reshape(-1, grad_win.shape[2])
-    stat_win = stat_win.reshape(-1, 16, tiles, TILE).transpose(0, 2, 1, 3).reshape(-1, 16, TILE)
-    query_low = query_back(bounds, q, k, v, mixed, mixed_grad, lse, own, window)
-    key_low, value_low = key_back(bounds, q, k, v, grad_win, stat_win, own, window)
+    query_low = query_back(bounds, q, k, v, grad_win, key_code, query_code, height)
+    key_low, value_low = key_back(bounds, q, k, v, grad_win, key_code, query_code, height)
 
     attn_part = (
         dot_nt(query_low, w_query) + dot_nt(key_low, w_key) + dot_nt(value_low, w_value)

time: 470 us -> 378 us (0.80)
  Pallas kernels: 302 us -> 226 us
  waiting for transfers between devices: 63.6 us -> 55.5 us
  other arithmetic: 29.1 us -> 23.7 us
    pallas_call x1, Pallas kernels: 83.1 us -> 53.3 us  [back_halo(): pl.pallas_call(back_halo_kernel, out_shape=(jax.ShapeDtypeStruct((blocks,...]
    pallas_call x3, Pallas kernels: 70.3 us -> 46.2 us  [local_call(): pl.pallas_call(kernel, grid_spec=grid, out_shape=out_shape, compiler_para...]
    pallas_call x1, Pallas kernels: 111 us -> 94 us  [ring_sum(): pl.pallas_call(functools.partial(ring_kernel, count), out_shape=tuple((ja...]
    unnamed x109 -> x117, local copies, waits for them, and re-layouts: 11.7 us -> 26.1 us
    ppermute x4, waiting for transfers between devices: 63.6 us -> 55.5 us  [swapped(): return lax.ppermute(value, 'tensor', [(0, 1), (1, 0)])]
    pallas_call x1, Pallas kernels: 38.2 us -> 32.3 us  [halo_qkv(): pl.pallas_call(halo_kernel, out_shape=(wide, wide, wide, jax.ShapeDtypeSt...]
  transfers between devices with their start and end apart: 4 -> 4, of which waited for: 4 -> 4; matrix products, arithmetic and copies ran while one was open for 5% -> 7% of each run, Pallas kernels for 0% -> 0%
where the time goes in v2:
time: 378 us; the launch traced here: 374 us
  Pallas kernels  226 us (60%)
  waiting for transfers between devices  55.5 us (15%)
  local copies, waits for them, and re-layouts  32.5 us (9%)
  matrix products  32 us (8%)
  other arithmetic  23.7 us (6%)
    pallas_call x1, Pallas kernels, ring_sum(): pl.pallas_call(functools.partial(ring_kernel, count), out_shape=tuple((ja...  94 us
    ppermute x4, waiting for transfers between devices, swapped(): return lax.ppermute(value, 'tensor', [(0, 1), (1, 0)])  55.5 us
    pallas_call x1, Pallas kernels, back_halo(): pl.pallas_call(back_halo_kernel, out_shape=(jax.ShapeDtypeStruct((blocks,...  53.3 us
    pallas_call x3, Pallas kernels, local_call(): pl.pallas_call(kernel, grid_spec=grid, out_shape=out_shape, compiler_para...  46.2 us
    pallas_call x1, Pallas kernels, halo_qkv(): pl.pallas_call(halo_kernel, out_shape=(wide, wide, wide, jax.ShapeDtypeSt...  32.3 us
    unnamed x117, local copies, waits for them, and re-layouts  26.1 us
    dot_general x6, matrix products, dot_nt(): lax.dot_general(left, right, (((1,), (1,)), ((), ())), preferred_element_...  11.6 us
    dot_general x6, matrix products, dot_tn(): lax.dot_general(left, right, (((0,), (0,)), ((), ())), preferred_element_...  11.3 us
  transfers between devices with their start and end apart: 4, of which 4 were waited for; matrix products, arithmetic and copies ran while one was open for 7% of the time, Pallas kernels for 0%

profile of v2, /device:TPU:0, one launch (start us, length us, event | category | flops | bytes accessed | tf_op | source)
XLA Modules:
  0.0 374.4 jit_solution(4737546401614379117)
XLA Ops:
  13.8 32.3 %halo_qkv.1 = (bf16[3840,384]{1,0:T(8,128)(2,1)S(1)}, bf16[3840,384]{1,0:T(8,128)(2,1)S(1)}, bf16[3840,384]{1,0:T(8,128)(2,1)S(1)}, bf16[768,768]{1,0:T(8,128)(2...) custom-call(bf16[768,768]{1,0:T(8,128)(2,1)S(1)} %copy-done.10, bf16[384,768]{1,0:T(8,128)(2,1)S(1)} %copy-done.8, ...), custom_call_target="tpu_custom_call" | custom-call | tf_op jit(solution)/shard_map/halo_qkv/pallas_call | solution.py:267
  48.2 17.9 %attend.1 = (bf16[768,384]{1,0:T(8,128)(2,1)}, f32[8,768]{1,0:T(8,128)S(1)}) custom-call(s32[2,3]{1,0:T(2,128)S(1)} %pad_add_fusion.b_ref, bf16[3840,384]{1,0:T(8,128)(2,1)S(1)} %get-tuple-element.33.q_ref, bf16[3840,384]{1,0:T(8,128)(2,1)S(1)} %get-tuple-element.34.k_ref, bf16[3840,384]{1,0:T(8,128)(2,1)S(1)} %get-tuple-element.35.v_ref, ...), custom_call_target="tpu_custom_call" | custom-call | tf_op jit(solution)/shard_map/attend/pallas_call | solution.py:536
  66.2 2.4 copy.49
  71.8 2.4 copy.51
  74.2 2.2 fusion.31
  76.8 2.1 fusion.30
  79.2 2.8 multiply_convert_fusion
  82.1 4.9 %convert_reduce_fusion = (f32[1536]{0:T(1024)}, bf16[768,1536]{1,0:T(8,128)(2,1)S(1)}) fusion(f32[768,1536]{1,0:T(8,128)S(1)} %get-tuple-element.112, f32[1536]{0:T(1024)S(1)} %convert_element_type.135, bf16[768,768]{1,0:T(8,128)(2,1)S(1)} %copy-done.38, bf16[1536,768]{1,0:T(8,128)(2,1)S(1)} %copy-done.51), kind=kOutput, calls=%fused_computation.7 | convolution fusion | flops 1827273216 | bytes 10629120 | tf_op jit(solution)/shard_map/dot_general | solution.py:38
  90.8 2.0 convolution_convert_fusion.3
  93.2 3.5 convolution_convert_fusion.1.refs_1_
  96.8 3.4 convolution_convert_fusion.refs_2_
  100.2 12.2 %collective-permute-done.2 = bf16[768,768]{0,1:T(8,128)(2,1)S(1)} collective-permute-done((bf16[768,768]{0,1:T(8,128)(2,1)S(1)}, bf16[768,768]{0,1:T(8,128)(2,1)S(1)}, u32[]{:S(2)}, u32[]{:S(2)}) %collective-permute-start.2) | collective-permute-done | bytes 1179680 | tf_op jit(solution)/shard_map/ppermute | solution.py:786
  114.2 23.5 %collective-permute-done.1 = bf16[768,768]{0,1:T(8,128)(2,1)S(1)} collective-permute-done((bf16[768,768]{0,1:T(8,128)(2,1)S(1)}, bf16[768,768]{0,1:T(8,128)(2,1)S(1)}, u32[]{:S(2)}, u32[]{:S(2)}) %collective-permute-start.1) | collective-permute-done | bytes 1179680 | tf_op jit(solution)/shard_map/ppermute | solution.py:786
  137.7 3.6 convert_reduce_fusion.3
  142.8 53.3 %back_halo.1 = (bf16[5,768,384]{2,1,0:T(8,128)(2,1)S(1)}, bf16[3840,128]{1,0:T(8,128)(2,1)S(1)}) custom-call(bf16[768,384]{1,0:T(8,128)(2,1)S(1)} %convolution_convert_fusion.8.x_ref, bf16[768,384]{1,0:T(8,128)(2,1)} %get-tuple-element.37.o_ref, f32[8,768]{1,0:T(8,128)S(1)} %get-tuple-element.39.lse_ref, bf16[3840,128]{1,0:T(8,128)(2,1)S(1)} %select_convert_fusion.kc_ref), custom_call_target="tpu_custom_call" | custom-call | tf_op jit(solution)/shard_map/back_halo/pallas_call | solution.py:415
  196.1 13.9 %query_back.1 = bf16[768,384]{1,0:T(8,128)(2,1)S(1)} custom-call(s32[2,3]{1,0:T(2,128)S(1)} %pad_add_fusion.b_ref, bf16[3840,384]{1,0:T(8,128)(2,1)S(1)} %copy-done.3, bf16[3840,384]{1,0:T(8,128)(2,1)S(1)} %copy-done.5, bf16[3840,384]{1,0:T(8,128)(2,1)S(1)} %copy-done.7, bf16[3840,384]{1,0:T(8,128)(2,1)S(1)} %bitcast.66, ...), custom_call_target="tpu_custom_call" | custom-call | tf_op jit(solution)/shard_map/query_back/pallas_call | solution.py:536
  210.0 14.4 %key_back.1 = (bf16[768,384]{1,0:T(8,128)(2,1)S(1)}, bf16[768,384]{1,0:T(8,128)(2,1)S(1)}) custom-call(s32[2,3]{1,0:T(2,128)S(1)} %pad_add_fusion.b_ref, bf16[3840,384]{1,0:T(8,128)(2,1)S(1)} %copy-done.3, bf16[3840,384]{1,0:T(8,128)(2,1)S(1)} %copy-done.5, bf16[3840,384]{1,0:T(8,128)(2,1)S(1)} %copy-done.7, bf16[3840,384]{1,0:T(8,128)(2,1)S(1)} %bitcast.67, ...), custom_call_target="tpu_custom_call" | custom-call | tf_op jit(solution)/shard_map/key_back/pallas_call | solution.py:536
  225.2 2.2 fusion.32
  238.2 19.4 %collective-permute-done.3 = bf16[768,768]{0,1:T(8,128)(2,1)S(1)} collective-permute-done((bf16[768,768]{0,1:T(8,128)(2,1)S(1)}, bf16[768,768]{0,1:T(8,128)(2,1)S(1)}, u32[]{:S(2)}, u32[]{:S(2)}) %collective-permute-start.3) | collective-permute-done | bytes 1179680 | tf_op jit(solution)/shard_map/ppermute | solution.py:786
  258.9 94.0 %ring_sum.1 = (bf16[768,1536]{1,0:T(8,128)(2,1)S(1)}, bf16[768,1536]{1,0:T(8,128)(2,1)S(1)}, bf16[1536,768]{1,0:T(8,128)(2,1)S(1)}, f32[128,128]{1,0:T(8,128)S(1)}) custom-call(bf16[768,1536]{1,0:T(8,128)(2,1)S(1)} %pad_maximum_fusion.refs_0_, bf16[768,1536]{1,0:T(8,128)(2,1)S(1)} %copy-done.11, bf16[1536,768]{1,0:T(8,128)(2,1)S(1)} %copy-done.12, ...), custom_call_target="tpu_custom_call" | custom-call | tf_op jit(solution)/shard_map/ring_sum/pallas_call | solution.py:768
  359.0 2.4 fusion.14
  361.4 3.2 copy.61
  368.6 2.8 convert_element_type.166
  371.4 2.5 convert_element_type.167
  (169 shorter events, 49.1 us)
Async XLA Ops:
  0.7 78.6 %copy-start = (bf16[768,1536]{1,0:T(8,128)(2,1)S(1)}, bf16[768,1536]{1,0:T(8,128)(2,1)}, u32[]{:S(2)}) copy-start(bf16[768,1536]{1,0:T(8,128)(2,1)} %param.31) | copy-start | bytes 7077892
  48.2 17.9 %copy-start.2 = (bf16[3840,384]{1,0:T(8,128)(2,1)}, bf16[3840,384]{1,0:T(8,128)(2,1)S(1)}, u32[]{:S(2)}) copy-start(bf16[3840,384]{1,0:T(8,128)(2,1)S(1)} %get-tuple-element.33.q_ref) | copy-start | bytes 8847364
  48.2 17.9 %copy-start.4 = (bf16[3840,384]{1,0:T(8,128)(2,1)}, bf16[3840,384]{1,0:T(8,128)(2,1)S(1)}, u32[]{:S(2)}) copy-start(bf16[3840,384]{1,0:T(8,128)(2,1)S(1)} %get-tuple-element.34.k_ref) | copy-start | bytes 8847364
  48.2 17.9 %copy-start.6 = (bf16[3840,384]{1,0:T(8,128)(2,1)}, bf16[3840,384]{1,0:T(8,128)(2,1)S(1)}, u32[]{:S(2)}) copy-start(bf16[3840,384]{1,0:T(8,128)(2,1)S(1)} %get-tuple-element.35.v_ref) | copy-start | bytes 8847364
  66.1 5.7 %copy-start.48 = (bf16[768]{0:T(1024)(128)(2,1)S(1)}, bf16[768]{0:T(1024)(128)(2,1)}, u32[]{:S(2)}) copy-start(bf16[768]{0:T(1024)(128)(2,1)} %param.30) | copy-start | bytes 4612
  66.1 5.7 %copy-start.49 = (bf16[768]{0:T(1024)(128)(2,1)S(1)}, bf16[768]{0:T(1024)(128)(2,1)}, u32[]{:S(2)}) copy-start(bf16[768]{0:T(1024)(128)(2,1)} %param.28) | copy-start | bytes 4612
  66.1 5.7 %copy-start.50 = (bf16[768]{0:T(1024)(128)(2,1)S(1)}, bf16[768]{0:T(1024)(128)(2,1)}, u32[]{:S(2)}) copy-start(bf16[768]{0:T(1024)(128)(2,1)} %param.34) | copy-start | bytes 4612
  66.1 5.7 %copy-start.46 = (bf16[1536]{0:T(1024)(128)(2,1)S(1)}, bf16[1536]{0:T(1024)(128)(2,1)}, u32[]{:S(2)}) copy-start(bf16[1536]{0:T(1024)(128)(2,1)} %param.32) | copy-start | bytes 9220
  66.1 10.7 %collective-permute-start = (bf16[768,384]{1,0:T(8,128)(2,1)}, bf16[768,384]{1,0:T(8,128)(2,1)}, u32[]{:S(2)}, u32[]{:S(2)}) collective-permute-start(bf16[768,384]{1,0:T(8,128)(2,1)} %get-tuple-element.37.o_ref), channel_id=1, source_target_pairs={{0,1},{1,0},{2,3},{3,2},{4,5},{5,4},{6,7},{7,6},{8,9},{9,8},{10,11... | collective-permute-start | bytes 1769480 | tf_op jit(solution)/shard_map/ppermute | solution.py:786
  89.0 23.4 %collective-permute-start.2 = (bf16[768,768]{0,1:T(8,128)(2,1)S(1)}, bf16[768,768]{0,1:T(8,128)(2,1)S(1)}, u32[]{:S(2)}, u32[]{:S(2)}) collective-permute-start(bf16[768,768]{0,1:T(8,128)(2,1)S(1)} %convolution_convert_fusion.2), channel_id=1, source_target_pairs={{0,1},{1,0},{2,3},{3,2},{4,5},{5,4},{6,7},{7,6},{8,9},{9,8},{10,11... | collective-permute-start | bytes 3538952 | tf_op jit(solution)/shard_map/ppermute | solution.py:786
  92.8 44.9 %collective-permute-start.1 = (bf16[768,768]{0,1:T(8,128)(2,1)S(1)}, bf16[768,768]{0,1:T(8,128)(2,1)S(1)}, u32[]{:S(2)}, u32[]{:S(2)}) collective-permute-start(bf16[768,768]{0,1:T(8,128)(2,1)S(1)} %convolution_convert_fusion.3), channel_id=1, source_target_pairs={{0,1},{1,0},{2,3},{3,2},{4,5},{5,4},{6,7},{7,6},{8,9},{9,8},{10,11... | collective-permute-start | bytes 3538952 | tf_op jit(solution)/shard_map/ppermute | solution.py:786
  100.2 37.5 %copy-start.36 = (bf16[768,768]{0,1:T(8,128)(2,1)S(1)}, bf16[768,768]{0,1:T(8,128)(2,1)}, u32[]{:S(2)}) copy-start(bf16[768,768]{0,1:T(8,128)(2,1)} %copy.51) | copy-start | bytes 3538948
  114.2 27.2 %copy-start.9 = (bf16[384,768]{1,0:T(8,128)(2,1)S(1)}, bf16[384,768]{1,0:T(8,128)(2,1)}, u32[]{:S(2)}) copy-start(bf16[384,768]{1,0:T(8,128)(2,1)} %wo_ref.1) | copy-start | bytes 1769476
  137.7 58.3 %copy-start.5 = (bf16[3840,384]{1,0:T(8,128)(2,1)S(1)}, bf16[3840,384]{1,0:T(8,128)(2,1)}, u32[]{:S(2)}) copy-start(bf16[3840,384]{1,0:T(8,128)(2,1)} %copy-done.4) | copy-start | bytes 8847364
  137.7 58.4 %copy-start.7 = (bf16[3840,384]{1,0:T(8,128)(2,1)S(1)}, bf16[3840,384]{1,0:T(8,128)(2,1)}, u32[]{:S(2)}) copy-start(bf16[3840,384]{1,0:T(8,128)(2,1)} %copy-done.6) | copy-start | bytes 8847364
  141.4 54.7 %copy-start.3 = (bf16[3840,384]{1,0:T(8,128)(2,1)S(1)}, bf16[3840,384]{1,0:T(8,128)(2,1)}, u32[]{:S(2)}) copy-start(bf16[3840,384]{1,0:T(8,128)(2,1)} %copy-done.2) | copy-start | bytes 8847364
  210.0 15.2 %copy-start.22 = (bf16[768,384]{1,0:T(8,128)(2,1)S(1)}, bf16[768,384]{1,0:T(8,128)(2,1)}, u32[]{:S(2)}) copy-start(bf16[768,384]{1,0:T(8,128)(2,1)} %wq_ref.1) | copy-start | bytes 1769476
  232.6 25.0 %collective-permute-start.3 = (bf16[768,768]{0,1:T(8,128)(2,1)S(1)}, bf16[768,768]{0,1:T(8,128)(2,1)S(1)}, u32[]{:S(2)}, u32[]{:S(2)}) collective-permute-start(bf16[768,768]{0,1:T(8,128)(2,1)S(1)} %add_convert_fusion), channel_id=1, source_target_pairs={{0,1},{1,0},{2,3},{3,2},{4,5},{5,4},{6,7},{7,6},{8,9},{9,8},{10,11... | collective-permute-start | bytes 3538952 | tf_op jit(solution)/shard_map/ppermute | solution.py:786
  237.9 19.6 %copy-start.32 = (bf16[768,768]{0,1:T(8,128)(2,1)S(1)}, bf16[768,768]{0,1:T(8,128)(2,1)}, u32[]{:S(2)}) copy-start(bf16[768,768]{0,1:T(8,128)(2,1)} %copy.49) | copy-start | bytes 3538948
  238.0 21.0 %copy-start.12 = (bf16[1536,768]{1,0:T(8,128)(2,1)S(1)}, bf16[1536,768]{1,0:T(8,128)(2,1)}, u32[]{:S(2)}) copy-start(bf16[1536,768]{1,0:T(8,128)(2,1)} %convolution_convert_fusion.refs_2_) | copy-start | bytes 7077892
  238.2 20.7 %copy-start.45 = (f32[1536]{0:T(1024)S(1)}, f32[1536]{0:T(1024)}, u32[]{:S(2)}) copy-start(f32[1536]{0:T(1024)} %get-tuple-element.113) | copy-start | bytes 18436
  238.2 20.7 %copy-start.42 = (f32[768]{0:T(1024)S(1)}, f32[768]{0:T(1024)}, u32[]{:S(2)}) copy-start(f32[768]{0:T(1024)} %get-tuple-element.83) | copy-start | bytes 9220
  238.2 20.7 %copy-start.41 = (f32[768]{0:T(1024)S(1)}, f32[768]{0:T(1024)}, u32[]{:S(2)}) copy-start(f32[768]{0:T(1024)} %get-tuple-element.89) | copy-start | bytes 9220
  238.2 20.7 %copy-start.11 = (bf16[768,1536]{1,0:T(8,128)(2,1)S(1)}, bf16[768,1536]{1,0:T(8,128)(2,1)}, u32[]{:S(2)}) copy-start(bf16[768,1536]{1,0:T(8,128)(2,1)} %convolution_convert_fusion.1.refs_1_) | copy-start | bytes 7077892
  (32 other events, 64.5 us)
